TPU v7x, 256 devices: a whole 4x4x8 slice. The times are simulated.
256 devices in a mesh: blk: 64 (over y_lo, x, z), states: 4 (over y_hi, core).
Axes of the slice: x: 4, y: 4 (y_hi: 2, y_lo: 2; y = y_hi * 2 + y_lo), z: 8, core: 2. Of those that a mesh axis runs over, the one named last changes fastest.
Arguments:
- start_states: float32 [128, 16, 128, 512], P('blk', None, None, 'states'), may hold values from -6 to 6
- couplings: float32 [16, 128, 128], replicated, may hold values from -0.1875 to 0.1875
- potential: float32 [128, 16, 128], P('blk'), may hold values from -18 to 18
- site_offsets: int32 [128, 6, 16], P('blk'), may hold values from 0 to 15
- coupling_index: int32 [128, 7, 16], P('blk'), may hold values from 0 to 15
- degrees: int32 [512], P('states'), may hold values from 1 to 3, as said below
Outputs:
- orthonormal: float32 [128, 16, 128, 512], P('blk', 'states')
Inputs may be any that keep to these rules, and one draw needn't show every extreme that they name: `degrees`: every degree from 1 to 3 belongs to some state.
All inputs are finite; a program needn't handle non-finite values.
Results may differ from a plain program's by a relative error of at most 0.0003.
Values sent between devices are 32-bit elements; how exact they have to be, the bound alone decides.
A program may use at most 128 MiB of HBM per device.

v0:
```python
import jax
import jax.numpy as jnp
from jax import lax
from jax.sharding import PartitionSpec as P

cut_share = 0.3
exact = lax.Precision.HIGHEST


def padded_2(shard, sides, width):
    for axis, dim in sides:
        devices, length = (lax.axis_size(axis), shard.shape[dim])
        up = [(i, (i + 1) % devices) for i in range(devices)]
        down = [(j, i) for i, j in up]
        last = lax.slice_in_dim(shard, length - width, length, axis=dim)
        first = lax.slice_in_dim(shard, 0, width, axis=dim)
        before = lax.ppermute(last, axis, up)
        after = lax.ppermute(first, axis, down)
        shard = jnp.concatenate([before, shard, after], axis=dim)
    return shard


def copy_for_each(shard, axis):
    copies = jnp.broadcast_to(shard, (lax.axis_size(axis), *shard.shape))
    return lax.all_to_all(copies, axis, split_axis=0, concat_axis=0, tiled=True)


def folded_in_pairs(pieces, combine):
    while len(jax.tree.leaves(pieces)[0]) > 1:
        pieces = jax.vmap(combine)(
            *(jax.tree.map(lambda part: part[side::2], pieces) for side in (0, 1))
        )
    return jax.tree.map(lambda part: part[0], pieces)


def joined_all(shard, axis, combine):
    pieces = jax.tree.map(lambda part: copy_for_each(part, axis), shard)
    return folded_in_pairs(pieces, combine)


def coupling_blocks(couplings, index_rows):
    return jnp.take(couplings, index_rows, axis=0)


def apply_inner(padded, blocks_used, onsite, offset_rows):
    middle = padded[1:-1]
    lower_layers = padded[:-2]
    upper_layers = padded[2:]
    count = onsite.shape[1]
    site_ids = jnp.arange(count, dtype=jnp.int32)
    layer_ids = jnp.arange(middle.shape[0], dtype=jnp.int32)
    pieces = [middle]
    for slot in range(1, 7):
        if slot == 5:
            source = lower_layers
        elif slot == 6:
            source = upper_layers
        else:
            source = middle
        neighbour = (site_ids[None, :] + offset_rows[:, slot - 1, :]) % count
        pieces.append(source[layer_ids[:, None], neighbour])
    stacked = jnp.stack(pieces, axis=1)
    summed = jnp.einsum("lksij,lksjn->lsin", blocks_used, stacked, precision=exact)
    return summed + onsite[..., None] * middle


def extrema_of(couplings, onsite, index_rows):
    row_abs = jnp.sum(jnp.abs(couplings), axis=2)
    diag_all = jnp.diagonal(couplings, axis1=1, axis2=2)
    table_ids = jnp.arange(couplings.shape[0], dtype=jnp.int32)
    onehot = (index_rows[..., None] == table_ids).astype(jnp.float32)
    picked_abs = jnp.einsum("lksc,ci->lksi", onehot, row_abs, precision=exact)
    picked_diag = jnp.einsum("lsc,ci->lsi", onehot[:, 0], diag_all, precision=exact)
    centers = picked_diag + onsite
    radii = picked_abs[:, 0] - jnp.abs(picked_diag) + jnp.sum(picked_abs[:, 1:], axis=1)
    return (jnp.max(centers + radii), jnp.min(centers - radii))


def combine(first, second):
    return (jnp.maximum(first[0], second[0]), jnp.minimum(first[1], second[1]))


def faces(field):
    return padded_2(field, (("blk", 0),), 1)


def per_device(start_states, couplings, potential, site_offsets, coupling_index, degrees):
    upper, lower = joined_all(extrema_of(couplings, potential, coupling_index), "blk", combine)
    cut_edge = lower + cut_share * (upper - lower)
    middle_value = (upper + cut_edge) / 2.0
    half_width = (upper - cut_edge) / 2.0

    def scaled(applied, field):
        return (applied - middle_value * field) / half_width

    local_blocks = coupling_blocks(couplings, coupling_index)
    first_step = scaled(
        apply_inner(faces(start_states), local_blocks, potential, site_offsets), start_states
    )
    second = (
        2.0
        * scaled(apply_inner(faces(first_step), local_blocks, potential, site_offsets), first_step)
        - start_states
    )
    third = (
        2.0 * scaled(apply_inner(faces(second), local_blocks, potential, site_offsets), second)
        - first_step
    )
    chosen = jnp.where(degrees == 1, first_step, jnp.where(degrees == 2, second, third))
    regrouped = lax.all_to_all(chosen, "states", split_axis=1, concat_axis=3, tiled=True)
    rows = regrouped.reshape(-1, regrouped.shape[-1])
    partial_gram = lax.dot_general(
        rows, rows, (((0,), (0,)), ((), ())), precision=exact, preferred_element_type=jnp.float32
    )
    gram = lax.psum(partial_gram, ("blk", "states"))
    factor = jnp.linalg.cholesky(gram)
    identity = jnp.eye(gram.shape[0], dtype=jnp.float32)
    inverse_factor = jax.scipy.linalg.solve_triangular(factor, identity, lower=True)
    orthonormal = jnp.dot(
        rows, inverse_factor.T, precision=exact, preferred_element_type=jnp.float32
    )
    return orthonormal.reshape(regrouped.shape)


def solution(mesh):
    in_specs = (
        P("blk", None, None, "states"),
        P(),
        P("blk", None, None),
        P("blk", None, None),
        P("blk", None, None),
        P("states"),
    )
    out_specs = P("blk", "states", None, None)
    return jax.shard_map(
        per_device, mesh=mesh, in_specs=in_specs, out_specs=out_specs, check_vma=False
    )
```

profile of v0, /device:TPU:1, one launch (start us, length us, event | category | flops | bytes accessed | tf_op | source)
XLA Modules:
  0.0 721.7 jit_solution(9385407167922655574)
XLA Ops:
  8.1 6.1 copy.46
  18.6 13.5 %all-to-all-start = ((f32[64,1,1]{2,1,0:T(1,128)}), f32[64,1,1]{2,1,0:T(1,128)S(1)}, u32[]{:S(2)}, u32[]{:S(2)}) async-start(f32[64,1,1]{2,1,0:T(1,128)} %broadcast_in_dim.49), calls=%async_computation | async-start | bytes 65536 | tf_op jit(solution)/shard_map/all_to_all | solution.py:25
  33.6 5.5 collective-permute-start.1
  58.9 6.7 gather_fusion
  67.0 8.0 %all-to-all-start.1 = ((f32[64,1,1]{2,1,0:T(1,128)}), f32[64,1,1]{2,1,0:T(1,128)S(1)}, u32[]{:S(2)}, u32[]{:S(2)}) async-start(f32[64,1,1]{2,1,0:T(1,128)} %broadcast_in_dim.50), calls=%async_computation.1 | async-start | bytes 65536 | tf_op jit(solution)/shard_map/all_to_all | solution.py:25
  76.8 7.4 %all-to-all-done.1 = f32[64,1,1]{2,1,0:T(1,128)S(1)} async-done(((f32[64,1,1]{2,1,0:T(1,128)}), f32[64,1,1]{2,1,0:T(1,128)S(1)}, u32[]{:S(2)}, u32[]{:S(2)}) %all-to-all-start.1) | async-done | bytes 288 | tf_op jit(solution)/shard_map/all_to_all | solution.py:25
  107.3 21.0 %bitcast_dynamic-update-slice_fusion.2 = (f32[2,7,16,128,128]{4,3,2,0,1:T(8,128)}, f32[2,16,128,128]{3,2,1,0:T(8,128)S(1)}) fusion(f32[]{:T(128)S(6)} %div.29, f32[2,16,128,128]{3,2,1,0:T(8,128)S(1)} %copy-done.1, f32[]{:T(128)S(6)} %div.28, f32[2,16,128]{2,1,0:T(8,128)S(1)} %copy-done.22, f32[2,7,16,128,128]{4,3,1,2,0:T(8,128)} %constant_dynamic-update-slice_fusion, ...), kind=kOutput, calls=%fused_computation.56 | convolution fusion | flops 5643436032 | bytes 35668200 | tf_op jit(solution)/shard_map/lksij,lksjn->lsin/dot_general | solution.py:63
  173.2 21.6 %bitcast_dynamic-update-slice_fusion.1 = (f32[2,7,16,128,128]{4,3,2,0,1:T(8,128)}, f32[2,16,128,128]{3,2,1,0:T(8,128)}) fusion(f32[2,16,128,128]{3,2,1,0:T(8,128)S(1)} %copy-done.1, f32[]{:T(128)S(6)} %div.29, f32[2,16,128,128]{3,2,1,0:T(8,128)} %copy-done.2, f32[]{:T(128)S(6)} %div.28, f32[2,16,128]{2,1,0:T(8,128)S(1)} %copy-done.22, ...), kind=kOutput, calls=%fused_computation.50 | convolution fusion | flops 5644484608 | bytes 37765352 | tf_op jit(solution)/shard_map/lksij,lksjn->lsin/dot_general | solution.py:63
  197.7 4.6 collective-permute-start.5
  221.3 6.1 collective-permute-done.4
  242.6 21.2 %fusion.19 = f32[2,16,128,128]{3,2,1,0:T(8,128)} fusion(f32[2,16,128,128]{3,2,1,0:T(8,128)S(1)} %copy-done.4, f32[2,16,128,128]{3,2,1,0:T(8,128)S(1)} %copy-done.6, f32[2,7,16,128,128]{4,3,2,0,1:T(8,128)} %constant_dynamic-update-slice_fusion.12, f32[2,7,16,128,128]{4,3,2,1,0:T(8,128)} %bitcast.190, pred[2,7,16]{1,2,0:T(8,128)(4,1)S(1)} %copy.43, ...), kind=kOutput, calls=%fused_computation.49 | convolution fusion | flops 5645533184 | bytes 35668456 | tf_op jit(solution)/shard_map/lksij,lksjn->lsin/dot_general | solution.py:63
  265.5 35.0 %all_to_all.33 = f32[2,16,128,128]{3,2,0,1:T(8,128)S(1)} all-to-all(f32[2,16,128,128]{3,2,0,1:T(8,128)S(1)} %copy.52), channel_id=1, replica_groups=mesh['blk'=64,'states'=4] {'states'}, dimensions={1} | all-to-all | bytes 4194304 | tf_op jit(solution)/shard_map/all_to_all | solution.py:110
  301.9 4.5 fusion.11
  310.9 244.9 %all-reduce.3.cloned.1.call-done = f32[512,512]{0,1:T(8,128)} async-done(((f32[512,512]{0,1:T(8,128)}), f32[512,512]{0,1:T(8,128)}) %all-reduce.3.cloned.1.call-update) | async-done | bytes 1048592 | tf_op jit(solution)/shard_map/psum | solution.py:115
  560.9 11.7 %cholesky.104 = f32[128,128]{1,0:T(8,128)S(1)} custom-call(f32[128,128]{1,0:T(8,128)S(1)} %cholesky.266), custom_call_target="Cholesky" | custom-call | tf_op jit(solution)/shard_map/jit(cholesky)/cholesky | solution.py:116
  572.8 9.8 %custom-call.31 = f32[1,128,128]{1,2,0:T(8,128)S(1)} custom-call(f32[1,128,128]{2,1,0:T(8,128)S(1)} %get-tuple-element.48), custom_call_target="InvertDiagBlocksLowerTriangular" | custom-call | tf_op jit(solution)/shard_map/jit(cholesky)/cholesky | solution.py:116
  585.1 11.7 %cholesky.217 = f32[128,128]{1,0:T(8,128)S(1)} custom-call(f32[128,128]{1,0:T(8,128)S(1)} %cholesky.270), custom_call_target="Cholesky" | custom-call | tf_op jit(solution)/shard_map/jit(cholesky)/cholesky | solution.py:116
  596.9 10.0 %custom-call.32 = f32[1,128,128]{1,2,0:T(8,128)S(1)} custom-call(f32[1,128,128]{2,1,0:T(8,128)S(1)} %get-tuple-element.45), custom_call_target="InvertDiagBlocksLowerTriangular" | custom-call | tf_op jit(solution)/shard_map/jit(cholesky)/cholesky | solution.py:116
  608.4 11.7 %cholesky.238 = f32[128,128]{1,0:T(8,128)S(1)} custom-call(f32[128,128]{1,0:T(8,128)S(1)} %cholesky.275), custom_call_target="Cholesky" | custom-call | tf_op jit(solution)/shard_map/jit(cholesky)/cholesky | solution.py:116
  620.1 9.8 %custom-call.33 = f32[1,128,128]{1,2,0:T(8,128)S(1)} custom-call(f32[1,128,128]{2,1,0:T(8,128)S(1)} %get-tuple-element.42), custom_call_target="InvertDiagBlocksLowerTriangular" | custom-call | tf_op jit(solution)/shard_map/jit(cholesky)/cholesky | solution.py:116
  631.4 11.7 %cholesky.255 = f32[128,128]{1,0:T(8,128)S(1)} custom-call(f32[128,128]{1,0:T(8,128)S(1)} %convolution_subtract_fusion.5), custom_call_target="Cholesky" | custom-call | tf_op jit(solution)/shard_map/jit(cholesky)/cholesky | solution.py:116
  649.1 13.9 %while.1 = (s32[]{:T(128)}, f32[512,512]{1,0:T(8,128)}, s32[4,2]{0,1:T(2,128)S(1)}, f32[4,128,128]{2,1,0:T(8,128)}, s32[]{:T(128)}) while((s32[]{:T(128)}, f32[512,512]{1,0:T(8,128)}, s32[4,2]{0,1:T(2,128)S(1)}, f32[4,128,128]{2,1,0:T(8,128)}, s32[]{:T(128)}) %tuple.46), condition=%wide.while_cond, body=%wide.while_body.sunk | while | flops 2 | bytes 132205 | solution.py:118
  663.0 40.1 %custom-call.34 = f32[4,128,128]{1,2,0:T(8,128)S(1)} custom-call(f32[4,128,128]{2,1,0:T(8,128)} %get-tuple-element.12), custom_call_target="InvertDiagBlocksLowerTriangular" | custom-call | tf_op jit(solution)/shard_map/jit(_solve_triangular)/triangular_solve | solution.py:118
  709.8 4.8 fusion.30
  (211 shorter events, 174.8 us)
Async XLA Ops:
  8.1 6.2 copy-start.23
  8.1 8.3 %copy-start.22 = (f32[2,16,128]{2,1,0:T(8,128)S(1)}, f32[2,16,128]{2,1,0:T(8,128)}, u32[]{:S(2)}) copy-start(f32[2,16,128]{2,1,0:T(8,128)} %param.8) | copy-start | bytes 49156
  8.1 23.9 %copy-start.1 = (f32[2,16,128,128]{3,2,1,0:T(8,128)S(1)}, f32[2,16,128,128]{3,2,1,0:T(8,128)}, u32[]{:S(2)}) copy-start(f32[2,16,128,128]{3,2,1,0:T(8,128)} %param.6) | copy-start | bytes 6291460
  18.6 47.2 %all-to-all-start = ((f32[64,1,1]{2,1,0:T(1,128)}), f32[64,1,1]{2,1,0:T(1,128)S(1)}, u32[]{:S(2)}, u32[]{:S(2)}) async-start(f32[64,1,1]{2,1,0:T(1,128)} %broadcast_in_dim.49), calls=%async_computation | async-start | bytes 65536 | tf_op jit(solution)/shard_map/all_to_all | solution.py:25
  33.6 56.1 %collective-permute-start.1 = (f32[1,16,128,128]{3,2,1,0:T(8,128)}, f32[1,16,128,128]{3,2,1,0:T(8,128)}, u32[]{:S(2)}, u32[]{:S(2)}) collective-permute-start(f32[1,16,128,128]{3,2,1,0:T(8,128)} %get-tuple-element.37), channel_id=1, source_target_pairs={{4,0},{8,4},{12,8},{16,12},{20,16},{24,20},{28,24},{32,28},{36,32}... | collective-permute-start | bytes 3145736 | tf_op jit(solution)/shard_map/ppermute | solution.py:18
  39.2 50.6 %collective-permute-start = (f32[1,16,128,128]{3,2,1,0:T(8,128)}, f32[1,16,128,128]{3,2,1,0:T(8,128)}, u32[]{:S(2)}, u32[]{:S(2)}) collective-permute-start(f32[1,16,128,128]{3,2,1,0:T(8,128)} %get-tuple-element.38), channel_id=1, source_target_pairs={{0,4},{4,8},{8,12},{12,16},{16,20},{20,24},{24,28},{28,32},{32,36}... | collective-permute-start | bytes 3145736 | tf_op jit(solution)/shard_map/ppermute | solution.py:17
  49.2 3.4 copy-start.8
  52.6 2.3 copy-start.9
  67.0 17.2 %all-to-all-start.1 = ((f32[64,1,1]{2,1,0:T(1,128)}), f32[64,1,1]{2,1,0:T(1,128)S(1)}, u32[]{:S(2)}, u32[]{:S(2)}) async-start(f32[64,1,1]{2,1,0:T(1,128)} %broadcast_in_dim.50), calls=%async_computation.1 | async-start | bytes 65536 | tf_op jit(solution)/shard_map/all_to_all | solution.py:25
  75.0 480.9 %all-reduce.3.cloned.1.call-start = ((), (), s32[]{:S(2)}) async-start(), calls=%async_computation.3 | async-start | bytes 2097152 | tf_op jit(solution)/shard_map/psum | solution.py:115
  130.3 25.7 %collective-permute-start.3 = (f32[1,16,128,128]{3,2,1,0:T(8,128)}, f32[1,16,128,128]{3,2,1,0:T(8,128)S(1)}, u32[]{:S(2)}, u32[]{:S(2)}) collective-permute-start(f32[1,16,128,128]{3,2,1,0:T(8,128)} %get-tuple-element.33), channel_id=1, source_target_pairs={{4,0},{8,4},{12,8},{16,12},{20,16},{24,20},{28,24},{32,28},{36,32}... | collective-permute-start | bytes 3145736 | tf_op jit(solution)/shard_map/ppermute | solution.py:18
  131.4 26.1 %collective-permute-start.2 = (f32[1,16,128,128]{3,2,1,0:T(8,128)}, f32[1,16,128,128]{3,2,1,0:T(8,128)}, u32[]{:S(2)}, u32[]{:S(2)}) collective-permute-start(f32[1,16,128,128]{3,2,1,0:T(8,128)} %get-tuple-element.34), channel_id=1, source_target_pairs={{0,4},{4,8},{8,12},{12,16},{16,20},{20,24},{24,28},{28,32},{32,36}... | collective-permute-start | bytes 3145736 | tf_op jit(solution)/shard_map/ppermute | solution.py:17
  146.6 3.3 copy-start.16
  154.5 3.0 copy-start.3
  168.3 3.3 copy-start.18
  194.8 7.7 %copy-start.25 = (s32[128]{0:T(128)S(1)}, s32[128]{0:T(128)}, u32[]{:S(2)}) copy-start(s32[128]{0:T(128)} %param.11) | copy-start | bytes 1540
  194.8 7.7 %copy-start.5 = (f32[2,16,128,128]{3,2,1,0:T(8,128)S(1)}, f32[2,16,128,128]{3,2,1,0:T(8,128)}, u32[]{:S(2)}) copy-start(f32[2,16,128,128]{3,2,1,0:T(8,128)} %get-tuple-element.64) | copy-start | bytes 6291460
  197.7 23.7 %collective-permute-start.5 = (f32[1,16,128,128]{3,2,1,0:T(8,128)}, f32[1,16,128,128]{3,2,1,0:T(8,128)}, u32[]{:S(2)}, u32[]{:S(2)}) collective-permute-start(f32[1,16,128,128]{3,2,1,0:T(8,128)} %get-tuple-element.29), channel_id=1, source_target_pairs={{4,0},{8,4},{12,8},{16,12},{20,16},{24,20},{28,24},{32,28},{36,32}... | collective-permute-start | bytes 3145736 | tf_op jit(solution)/shard_map/ppermute | solution.py:18
  202.3 25.1 %collective-permute-start.4 = (f32[1,16,128,128]{3,2,1,0:T(8,128)S(1)}, f32[1,16,128,128]{3,2,1,0:T(8,128)}, u32[]{:S(2)}, u32[]{:S(2)}) collective-permute-start(f32[1,16,128,128]{3,2,1,0:T(8,128)S(1)} %get-tuple-element.30), channel_id=1, source_target_pairs={{0,4},{4,8},{8,12},{12,16},{16,20},{20,24},{24,28},{28,32},{32,36}... | collective-permute-start | bytes 3145736 | tf_op jit(solution)/shard_map/ppermute | solution.py:17
  210.6 3.3 copy-start.14
  239.6 3.0 copy-start.6
  301.9 4.5 copy-start.7
  555.8 2.6 copy-start.19
  649.1 57.0 %copy-start.20 = (f32[512,512]{1,0:T(8,128)S(1)}, f32[512,512]{1,0:T(8,128)}, u32[]{:S(2)}) copy-start(f32[512,512]{1,0:T(8,128)} %fusion.46) | copy-start | bytes 3145732
  (11 other events, 22.6 us)
Sparse Core Ops, SparseCore 0:
  306.6 249.1 all-reduce.2
where the time goes:
time: 730 us; the launch traced here: 722 us
  waiting for transfers between devices  261 us (36%)
  local copies, waits for them, and re-layouts  148 us (20%)
  other arithmetic  138 us (19%)
  matrix products  86.3 us (12%)
  blocking collectives  35 us (5%)
  starting transfers between devices  33.8 us (5%)
  between operations  19.3 us (3%)
    psum x1, waiting for transfers between devices, per_device(): gram = lax.psum(partial_gram, ('blk', 'states'))  245 us
    another operation x14, other arithmetic, per_device(): factor = jnp.linalg.cholesky(gram)  78.6 us
    dot_general x3, matrix products, apply_inner(): jnp.einsum('lksij,lksjn->lsin', blocks_used, stacked, precision=exact)  63.8 us
    gather x18, local copies, waits for them, and re-layouts, apply_inner(): pieces.append(source[layer_ids[:, None], neighbour])  50.7 us
    unnamed x69, local copies, waits for them, and re-layouts  47.6 us
    another operation x3, other arithmetic, per_device(): jax.scipy.linalg.solve_triangular(factor, identity, lower=True)  41.4 us
    all_to_all x1, blocking collectives, per_device(): lax.all_to_all(chosen, 'states', split_axis=1, concat_axis=3, tiled=True)  35 us
    all_to_all x2, starting transfers between devices, copy_for_each(): return lax.all_to_all(copies, axis, split_axis=0, concat_axis=0, tiled=True)  21.5 us
  transfers between devices with their start and end apart: 9, of which 5 were waited for; matrix products, arithmetic and copies ran while one was open for 10% of the time, Pallas kernels for 0%

commit v1 on v0

--- a/solution.py
+++ b/solution.py
@@ -1,10 +1,228 @@
+import functools
 import jax
 import jax.numpy as jnp
 from jax import lax
+from jax.experimental import pallas as pl
+from jax.experimental.pallas import tpu as pltpu
 from jax.sharding import PartitionSpec as P
 
 cut_share = 0.3
+
+MESH = pl.DeviceIdType.MESH
+F32 = jnp.float32
+BF16 = jnp.bfloat16
 exact = lax.Precision.HIGHEST
+VMEM_LIMIT = 60 * 1024 * 1024
+
+
+def place():
+    b, st = lax.axis_index("blk"), lax.axis_index("states")
+    z = lax.rem(b, 8)
+    x = lax.rem(lax.div(b, 8), 4)
+    y = lax.div(st, 2) * 2 + lax.div(b, 32)
+    return x, y, z, lax.rem(st, 2)
+
+
+def device(x, y, z, core):
+    return ((lax.rem(y, 2) * 4 + x) * 8 + z, lax.div(y, 2) * 2 + core)
+
+
+def greet(peers):
+    barrier = pltpu.get_barrier_semaphore()
+    for peer in peers:
+        pl.semaphore_signal(barrier, inc=1, device_id=peer, device_id_type=MESH)
+    pl.semaphore_wait(barrier, len(peers))
+
+
+def send(src, dst, send_sem, recv_sem, peer):
+    copy = pltpu.make_async_remote_copy(
+        src_ref=src, dst_ref=dst, send_sem=send_sem, recv_sem=recv_sem, device_id=peer, device_id_type=MESH
+    )
+    copy.start()
+    return copy
+
+
+def rows_at(start, size):
+    return pl.ds(pl.multiple_of(start, 8), size)
+
+
+def sum_kernel(g_ref, out_ref, r1, a1, r2, a2, r3, zbuf, gbuf, send_sems, recv_sems):
+    x, y, z, core = place()
+    core_peer = device(x, y, z, 1 - core)
+    x_peers = [device(lax.rem(x + d, 4), y, z, core) for d in (1, 2, 3)]
+    y_peers = [device(x, lax.rem(y + d, 4), z, core) for d in (1, 2, 3)]
+    z_peers = [device(x, y, lax.rem(z + d, 8), core) for d in range(1, 8)]
+    greet([core_peer] + x_peers + y_peers + z_peers)
+    used = iter(range(21))
+
+    def sems():
+        i = next(used)
+        return send_sems.at[i], recv_sems.at[i]
+
+    send(g_ref.at[rows_at((1 - core) * 640, 640)], r1, *sems(), core_peer).wait()
+    a1[...] = g_ref[rows_at(core * 640, 640)] + r1[...]
+    copies = [
+        send(a1.at[rows_at(lax.rem(x + d, 4) * 160, 160)], r2.at[d - 1], *sems(), x_peers[d - 1]) for d in (1, 2, 3)
+    ]
+    for copy in copies:
+        copy.wait()
+    a2[...] = (a1[rows_at(x * 160, 160)] + r2[0]) + (r2[1] + r2[2])
+    copies = [
+        send(a2.at[rows_at(lax.rem(y + d, 4) * 40, 40)], r3.at[d - 1], *sems(), y_peers[d - 1]) for d in (1, 2, 3)
+    ]
+    for copy in copies:
+        copy.wait()
+    zbuf[z] = (a2[rows_at(y * 40, 40)] + r3[0]) + (r3[1] + r3[2])
+    copies = [send(zbuf.at[z], zbuf.at[z], *sems(), z_peers[d - 1]) for d in range(1, 8)]
+    for copy in copies:
+        copy.wait()
+    own = rows_at(core * 640 + x * 160 + y * 40, 40)
+    gbuf[own] = ((zbuf[0] + zbuf[1]) + (zbuf[2] + zbuf[3])) + ((zbuf[4] + zbuf[5]) + (zbuf[6] + zbuf[7]))
+    copies = [send(gbuf.at[own], gbuf.at[own], *sems(), peer) for peer in y_peers]
+    for copy in copies:
+        copy.wait()
+    own = rows_at(core * 640 + x * 160, 160)
+    copies = [send(gbuf.at[own], gbuf.at[own], *sems(), peer) for peer in x_peers]
+    for copy in copies:
+        copy.wait()
+    own = rows_at(core * 640, 640)
+    send(gbuf.at[own], gbuf.at[own], *sems(), core_peer).wait()
+    out_ref[...] = gbuf[...]
+
+
+def sum_over_devices(packed):
+    vmem = pl.BlockSpec(memory_space=pltpu.VMEM)
+    return pl.pallas_call(
+        sum_kernel,
+        out_shape=jax.ShapeDtypeStruct((1280, 128), F32),
+        in_specs=[vmem],
+        out_specs=vmem,
+        scratch_shapes=[
+            pltpu.VMEM((640, 128), F32),
+            pltpu.VMEM((640, 128), F32),
+            pltpu.VMEM((3, 160, 128), F32),
+            pltpu.VMEM((160, 128), F32),
+            pltpu.VMEM((3, 40, 128), F32),
+            pltpu.VMEM((8, 40, 128), F32),
+            pltpu.VMEM((1280, 128), F32),
+            pltpu.SemaphoreType.DMA((21,)),
+            pltpu.SemaphoreType.DMA((21,)),
+        ],
+        compiler_params=pltpu.CompilerParams(collective_id=1, has_side_effects=True),
+        name="gram_sum",
+    )(packed)
+
+
+PAIRS = [(i, j) for i in range(4) for j in range(i + 1)]
+SLOT = {pair: n for n, pair in enumerate(PAIRS)}
+
+
+def halves(v):
+    hi = v.astype(BF16)
+    return hi, (v - hi.astype(F32)).astype(BF16)
+
+
+def thirds(v):
+    hi = v.astype(BF16).astype(F32)
+    rest = v - hi
+    mid = rest.astype(BF16).astype(F32)
+    return hi, mid, rest - mid
+
+
+def dot_nt(a, b):
+    return lax.dot_general(a, b, (((1,), (1,)), ((), ())), precision=exact, preferred_element_type=F32)
+
+
+def dot_nn(a, b):
+    return lax.dot_general(a, b, (((1,), (0,)), ((), ())), precision=exact, preferred_element_type=F32)
+
+
+def eliminate(work):
+    row = lax.broadcasted_iota(jnp.int32, (8, 128), 0)
+    for p in range(16):
+        lo = 8 * p
+        left, right = work[lo : lo + 8, :128], work[lo : lo + 8, 128:]
+        cols = [jnp.broadcast_to(left[:, lo + c : lo + c + 1], (8, 128)) for c in range(8)]
+        for j in range(8):
+            scale = lax.rsqrt(jnp.broadcast_to(cols[j][j : j + 1, :], (8, 128)))
+            lrow = jnp.broadcast_to(left[j : j + 1, :], (8, 128)) * scale
+            rrow = jnp.broadcast_to(right[j : j + 1, :], (8, 128)) * scale
+            factor = jnp.where(row > j, cols[j] * scale, 0.0)
+            for c in range(j + 1, 8):
+                cols[c] = cols[c] - factor * (jnp.broadcast_to(cols[c][j : j + 1, :], (8, 128)) * scale)
+            left = jnp.where(row == j, lrow, left - factor * lrow)
+            right = jnp.where(row == j, rrow, right - factor * rrow)
+        work[lo : lo + 8, :128] = left
+        work[lo : lo + 8, 128:] = right
+        if p < 15:
+            h, m, l = thirds(jnp.concatenate([left, right], axis=1))
+            lhs = jnp.concatenate([h[:, :128], h[:, :128], m[:, :128], m[:, :128], h[:, :128], l[:, :128]], axis=0).astype(BF16)
+            rhs = jnp.concatenate([h, m, h, m, l, h], axis=0).astype(BF16)
+            change = lax.dot_general(lhs, rhs, (((0,), (0,)), ((), ())), preferred_element_type=F32)
+            work[lo + 8 :, :] = work[lo + 8 :, :] - change[lo + 8 :, :]
+
+
+def factor_kernel(g_ref, x_ref, out_ref, blocks, work, low, inv, xh, xl, ih, il):
+    blocks[...] = g_ref[...]
+    inv[...] = jnp.zeros_like(inv)
+    xh[...], xl[...] = halves(x_ref[...])
+    eye = (lax.broadcasted_iota(jnp.int32, (128, 128), 0) == lax.broadcasted_iota(jnp.int32, (128, 128), 1)).astype(F32)
+
+    @pl.loop(0, 4)
+    def _(k):
+        work[:, :128] = blocks[lax.div(k * (k + 1), 2) + k]
+        work[:, 128:] = eye
+        eliminate(work)
+        for n in range(4):
+
+            @pl.when(k == n)
+            def _():
+                here = slice(128 * n, 128 * n + 128)
+                w = work[:, 128:]
+                inv[here, here] = w
+                if n > 0:
+                    known = dot_nn(low[here, : 128 * n], inv[: 128 * n, : 128 * n])
+                    inv[here, : 128 * n] = -dot_nn(w, known)
+                for i in range(n + 1, 4):
+                    low[128 * i : 128 * i + 128, here] = dot_nt(blocks[SLOT[i, n]], w)
+                for j in range(n + 1, 4):
+                    for i in range(j, 4):
+                        blocks[SLOT[i, j]] = blocks[SLOT[i, j]] - dot_nt(
+                            low[128 * i : 128 * i + 128, here], low[128 * j : 128 * j + 128, here]
+                        )
+
+    ih[...], il[...] = halves(inv[...])
+
+    def nt(a, b):
+        return lax.dot_general(a, b, (((1,), (1,)), ((), ())), preferred_element_type=F32)
+
+    for i in range(4):
+        here, upto = slice(128 * i, 128 * i + 128), 128 * i + 128
+        a, b = xh[:, :upto], xl[:, :upto]
+        u, v = ih[here, :upto], il[here, :upto]
+        out_ref[:, here] = nt(a, u) + (nt(a, v) + nt(b, u))
+
+
+def orthonormalised(packed, rows):
+    vmem = pl.BlockSpec(memory_space=pltpu.VMEM)
+    return pl.pallas_call(
+        factor_kernel,
+        out_shape=jax.ShapeDtypeStruct((1024, 512), F32),
+        in_specs=[vmem, vmem],
+        out_specs=vmem,
+        scratch_shapes=[
+            pltpu.VMEM((10, 128, 128), F32),
+            pltpu.VMEM((128, 256), F32),
+            pltpu.VMEM((512, 512), F32),
+            pltpu.VMEM((512, 512), F32),
+            pltpu.VMEM((1024, 512), BF16),
+            pltpu.VMEM((1024, 512), BF16),
+            pltpu.VMEM((512, 512), BF16),
+            pltpu.VMEM((512, 512), BF16),
+        ],
+        compiler_params=pltpu.CompilerParams(vmem_limit_bytes=VMEM_LIMIT),
+        name="factor",
+    )(packed.reshape(10, 128, 128), rows)
 
 
 def padded_2(shard, sides, width):
@@ -112,14 +330,11 @@
     partial_gram = lax.dot_general(
         rows, rows, (((0,), (0,)), ((), ())), precision=exact, preferred_element_type=jnp.float32
     )
-    gram = lax.psum(partial_gram, ("blk", "states"))
-    factor = jnp.linalg.cholesky(gram)
-    identity = jnp.eye(gram.shape[0], dtype=jnp.float32)
-    inverse_factor = jax.scipy.linalg.solve_triangular(factor, identity, lower=True)
-    orthonormal = jnp.dot(
-        rows, inverse_factor.T, precision=exact, preferred_element_type=jnp.float32
-    )
-    return orthonormal.reshape(regrouped.shape)
+    packed = jnp.concatenate(
+        [partial_gram[128 * i : 128 * i + 128, 128 * j : 128 * j + 128] for i, j in PAIRS], axis=0
+    )
+    gram = sum_over_devices(packed)
+    return orthonormalised(gram, rows).reshape(regrouped.shape)
 
 
 def solution(mesh):

time: 730 us -> 381 us (0.52)
  waiting for transfers between devices: 261 us -> 16.6 us
  other arithmetic: 138 us -> 14.9 us
  Pallas kernels: 0 us -> 67.7 us
  matrix products: 86.3 us -> 68.9 us
  between operations: 19.3 us -> 3.21 us
  local copies, waits for them, and re-layouts: 148 us -> 133 us
    psum x1 -> x0, waiting for transfers between devices: 245 us -> none  [per_device(): gram = lax.psum(partial_gram, ('blk', 'states'))]
    another operation x17 -> x0, other arithmetic: 120 us -> none  [the longest x14 78.6 us: per_device(): factor = jnp.linalg.cholesky(gram)]
    pallas_call x0 -> x2, Pallas kernels: none -> 67.7 us  [the longest x1 34.2 us: sum_over_devices(): pl.pallas_call(sum_kernel, out_shape=jax.ShapeDtypeStruct((1280, 128), F3...]
    another operation x17 -> x0, local copies, waits for them, and re-layouts: 14.1 us -> none
    another operation x13 -> x0, matrix products: 12.1 us -> none  [the longest x7 6.59 us: per_device(): jax.scipy.linalg.solve_triangular(factor, identity, lower=True)]
    unnamed x69 -> x68, local copies, waits for them, and re-layouts: 47.6 us -> 49.4 us
  transfers between devices with their start and end apart: 9 -> 8, of which waited for: 5 -> 4; matrix products, arithmetic and copies ran while one was open for 10% -> 19% of each run, Pallas kernels for 0% -> 0%
where the time goes in v1:
time: 381 us; the launch traced here: 374 us
  local copies, waits for them, and re-layouts  133 us (35%)
  matrix products  68.9 us (18%)
  Pallas kernels  67.7 us (18%)
  blocking collectives  35.3 us (9%)
  starting transfers between devices  34.2 us (9%)
  waiting for transfers between devices  16.6 us (4%)
  other arithmetic  14.9 us (4%)
    dot_general x3, matrix products, apply_inner(): jnp.einsum('lksij,lksjn->lsin', blocks_used, stacked, precision=exact)  64.3 us
    gather x18, local copies, waits for them, and re-layouts, apply_inner(): pieces.append(source[layer_ids[:, None], neighbour])  52.1 us
    unnamed x68, local copies, waits for them, and re-layouts  49.4 us
    all_to_all x1, blocking collectives, per_device(): lax.all_to_all(chosen, 'states', split_axis=1, concat_axis=3, tiled=True)  35.3 us
    pallas_call x1, Pallas kernels, sum_over_devices(): pl.pallas_call(sum_kernel, out_shape=jax.ShapeDtypeStruct((1280, 128), F3...  34.2 us
    pallas_call x1, Pallas kernels, orthonormalised(): pl.pallas_call(factor_kernel, out_shape=jax.ShapeDtypeStruct((1024, 512),...  33.5 us
    all_to_all x2, starting transfers between devices, copy_for_each(): return lax.all_to_all(copies, axis, split_axis=0, concat_axis=0, tiled=True)  21.9 us
    concatenate x3, other arithmetic, padded_2(): shard = jnp.concatenate([before, shard, after], axis=dim)  12 us
  transfers between devices with their start and end apart: 8, of which 4 were waited for; matrix products, arithmetic and copies ran while one was open for 19% of the time, Pallas kernels for 0%

profile of v1, /device:TPU:1, one launch (start us, length us, event | category | flops | bytes accessed | tf_op | source)
XLA Modules:
  0.0 374.0 jit_solution(15735465967860259089)
XLA Ops:
  1.6 6.2 %copy.40 = f32[16,128,128]{0,2,1:T(8,128)} copy(f32[16,128,128]{2,1,0:T(8,128)} %param.7) | data formatting | bytes 2097152 | tf_op args[1]
  12.1 13.5 %all-to-all-start = ((f32[64,1,1]{2,1,0:T(1,128)}), f32[64,1,1]{2,1,0:T(1,128)S(1)}, u32[]{:S(2)}, u32[]{:S(2)}) async-start(f32[64,1,1]{2,1,0:T(1,128)} %broadcast_in_dim.48), calls=%async_computation | async-start | bytes 65536 | tf_op jit(solution)/shard_map/all_to_all | solution.py:243
  27.1 5.5 %collective-permute-start.1 = (f32[1,16,128,128]{3,2,1,0:T(8,128)}, f32[1,16,128,128]{3,2,1,0:T(8,128)}, u32[]{:S(2)}, u32[]{:S(2)}) collective-permute-start(f32[1,16,128,128]{3,2,1,0:T(8,128)} %get-tuple-element.17), channel_id=1, source_target_pairs={{4,0},{8,4},{12,8},{16,12},{20,16},{24,20},{28,24},{32,28},{36,32}... | collective-permute-start | bytes 3145736 | tf_op jit(solution)/shard_map/ppermute | solution.py:236
  52.4 6.7 %gather_fusion = f32[224,128,128]{2,1,0:T(8,128)} fusion(f32[16,128,128]{2,1,0:T(8,128)S(1)} %copy-done, s32[1024]{0:T(1024)S(1)} %pad_clamp_fusion), kind=kCustom, calls=%fused_computation | custom fusion | bytes 29361024 | tf_op jit(solution)/shard_map/jit(_take)/gather | solution.py:260
  60.5 8.4 %all-to-all-start.1 = ((f32[64,1,1]{2,1,0:T(1,128)}), f32[64,1,1]{2,1,0:T(1,128)S(1)}, u32[]{:S(2)}, u32[]{:S(2)}) async-start(f32[64,1,1]{2,1,0:T(1,128)} %broadcast_in_dim.49), calls=%async_computation.1 | async-start | bytes 65536 | tf_op jit(solution)/shard_map/all_to_all | solution.py:243
  70.6 7.7 %all-to-all-done.1 = f32[64,1,1]{2,1,0:T(1,128)S(1)} async-done(((f32[64,1,1]{2,1,0:T(1,128)}), f32[64,1,1]{2,1,0:T(1,128)S(1)}, u32[]{:S(2)}, u32[]{:S(2)}) %all-to-all-start.1) | async-done | bytes 288 | tf_op jit(solution)/shard_map/all_to_all | solution.py:243
  83.6 3.9 %pad_maximum_fusion.4 = (f32[2,16,128,128]{3,2,1,0:T(8,128)}, f32[2,16,128,128]{3,2,1,0:T(8,128)}) fusion(f32[1,16,128,128]{3,2,1,0:T(8,128)} %collective-permute-done.1, f32[2,16,128,128]{3,2,1,0:T(8,128)S(1)} %copy-done.1, f32[1,16,128,128]{3,2,1,0:T(8,128)} %collective-permute-done), kind=kLoop, calls=%fused_computation.37 | loop fusion | flops 1048576 | bytes 8388608 | tf_op jit(solution)/shard_map/concatenate | solution.py:237
  87.5 3.6 gather_fusion.5
  94.3 3.6 gather_fusion.6
  101.1 21.4 %bitcast_dynamic-update-slice_fusion.1 = (f32[2,7,16,128,128]{4,3,2,0,1:T(8,128)}, f32[2,16,128,128]{3,2,1,0:T(8,128)}) fusion(f32[]{:T(128)S(6)} %div.21, f32[2,16,128,128]{3,2,1,0:T(8,128)S(1)} %copy-done.1, f32[]{:T(128)S(6)} %div.20, f32[2,16,128]{2,1,0:T(8,128)S(1)} %copy-done.17, f32[2,7,16,128,128]{4,3,1,2,0:T(8,128)} %constant_dynamic-update-slice_fusion, ...), kind=kOutput, calls=%fused_computation.52 | convolution fusion | flops 5643436032 | bytes 35668200 | tf_op jit(solution)/shard_map/lksij,lksjn->lsin/dot_general | solution.py:281
  130.5 3.6 gather_fusion.9
  134.1 3.6 gather_fusion.10
  137.7 3.6 gather_fusion.11
  152.1 4.0 %pad_maximum_fusion.2 = (f32[2,16,128,128]{3,2,1,0:T(8,128)}, f32[2,16,128,128]{3,2,1,0:T(8,128)}) fusion(f32[1,16,128,128]{3,2,1,0:T(8,128)} %collective-permute-done.3, f32[2,16,128,128]{3,2,1,0:T(8,128)S(1)} %copy-done.2, f32[1,16,128,128]{3,2,1,0:T(8,128)} %collective-permute-done.2), kind=kLoop, calls=%fused_computation.35 | loop fusion | flops 1048576 | bytes 8388608 | tf_op jit(solution)/shard_map/concatenate | solution.py:237
  156.1 3.6 gather_fusion.12
  168.1 21.6 %bitcast_dynamic-update-slice_fusion = (f32[2,7,16,128,128]{4,3,2,0,1:T(8,128)}, f32[2,16,128,128]{3,2,1,0:T(8,128)}) fusion(f32[2,16,128,128]{3,2,1,0:T(8,128)S(1)} %copy-done.1, f32[]{:T(128)S(6)} %div.21, f32[2,16,128,128]{3,2,1,0:T(8,128)} %get-tuple-element.32, f32[]{:T(128)S(6)} %div.20, f32[2,16,128]{2,1,0:T(8,128)S(1)} %copy-done.17, ...), kind=kOutput, calls=%fused_computation.46 | convolution fusion | flops 5644484608 | bytes 37765352 | tf_op jit(solution)/shard_map/lksij,lksjn->lsin/dot_general | solution.py:281
  193.1 4.9 %collective-permute-start.5 = (f32[1,16,128,128]{3,2,1,0:T(8,128)}, f32[1,16,128,128]{3,2,1,0:T(8,128)}, u32[]{:S(2)}, u32[]{:S(2)}) collective-permute-start(f32[1,16,128,128]{3,2,1,0:T(8,128)} %get-tuple-element.9), channel_id=1, source_target_pairs={{4,0},{8,4},{12,8},{16,12},{20,16},{24,20},{28,24},{32,28},{36,32}... | collective-permute-start | bytes 3145736 | tf_op jit(solution)/shard_map/ppermute | solution.py:236
  217.0 6.3 %collective-permute-done.4 = f32[1,16,128,128]{3,2,1,0:T(8,128)} collective-permute-done((f32[1,16,128,128]{3,2,1,0:T(8,128)}, f32[1,16,128,128]{3,2,1,0:T(8,128)}, u32[]{:S(2)}, u32[]{:S(2)}) %collective-permute-start.4) | collective-permute-done | bytes 1048608 | tf_op jit(solution)/shard_map/ppermute | solution.py:235
  223.3 4.0 %pad_maximum_fusion = (f32[2,16,128,128]{3,2,1,0:T(8,128)}, f32[2,16,128,128]{3,2,1,0:T(8,128)}) fusion(f32[1,16,128,128]{3,2,1,0:T(8,128)} %collective-permute-done.5, f32[2,16,128,128]{3,2,1,0:T(8,128)S(1)} %copy-done.4, f32[1,16,128,128]{3,2,1,0:T(8,128)} %collective-permute-done.4), kind=kLoop, calls=%fused_computation.33 | loop fusion | flops 1048576 | bytes 8388608 | tf_op jit(solution)/shard_map/concatenate | solution.py:237
  227.3 3.6 gather_fusion.18
  240.2 21.2 %fusion.16 = f32[2,16,128,128]{3,2,1,0:T(8,128)} fusion(f32[2,16,128,128]{3,2,1,0:T(8,128)S(1)} %copy-done.3, f32[2,16,128,128]{3,2,1,0:T(8,128)S(1)} %copy-done.4, f32[2,7,16,128,128]{4,3,2,0,1:T(8,128)} %constant_dynamic-update-slice_fusion.12, f32[2,7,16,128,128]{4,3,2,1,0:T(8,128)} %bitcast.138, pred[2,7,16]{1,2,0:T(8,128)(4,1)S(1)} %copy.37, ...), kind=kOutput, calls=%fused_computation.45 | convolution fusion | flops 5645533184 | bytes 35668456 | tf_op jit(solution)/shard_map/lksij,lksjn->lsin/dot_general | solution.py:281
  263.2 35.3 %all_to_all.33 = f32[2,16,128,128]{3,2,0,1:T(8,128)S(1)} all-to-all(f32[2,16,128,128]{3,2,0,1:T(8,128)S(1)} %copy.46), channel_id=1, replica_groups=mesh['blk'=64,'states'=4] {'states'}, dimensions={1} | all-to-all | bytes 4194304 | tf_op jit(solution)/shard_map/all_to_all | solution.py:328
  305.9 34.2 %gram_sum.1 = f32[1280,128]{1,0:T(8,128)} custom-call(f32[1280,128]{1,0:T(8,128)} %copy-done.16), custom_call_target="tpu_custom_call" | custom-call | tf_op jit(solution)/shard_map/gram_sum/pallas_call | solution.py:95
  340.1 33.5 %factor.1 = f32[1024,512]{1,0:T(8,128)} custom-call(f32[10,128,128]{2,1,0:T(8,128)} %bitcast.161, f32[1024,512]{1,0:T(8,128)} %bitcast.139), custom_call_target="tpu_custom_call" | custom-call | tf_op jit(solution)/shard_map/factor/pallas_call | solution.py:208
  (155 shorter events, 107.1 us)
Async XLA Ops:
  1.6 6.2 %copy-start.18 = (s32[2,7,16]{2,0,1:T(2,128)S(1)}, s32[2,7,16]{2,0,1:T(2,128)}, u32[]{:S(2)}) copy-start(s32[2,7,16]{2,0,1:T(2,128)} %param.10) | copy-start | bytes 2692
  1.6 8.4 %copy-start.17 = (f32[2,16,128]{2,1,0:T(8,128)S(1)}, f32[2,16,128]{2,1,0:T(8,128)}, u32[]{:S(2)}) copy-start(f32[2,16,128]{2,1,0:T(8,128)} %param.8) | copy-start | bytes 49156
  1.6 24.0 %copy-start.1 = (f32[2,16,128,128]{3,2,1,0:T(8,128)S(1)}, f32[2,16,128,128]{3,2,1,0:T(8,128)}, u32[]{:S(2)}) copy-start(f32[2,16,128,128]{3,2,1,0:T(8,128)} %param.6) | copy-start | bytes 6291460
  12.1 47.0 %all-to-all-start = ((f32[64,1,1]{2,1,0:T(1,128)}), f32[64,1,1]{2,1,0:T(1,128)S(1)}, u32[]{:S(2)}, u32[]{:S(2)}) async-start(f32[64,1,1]{2,1,0:T(1,128)} %broadcast_in_dim.48), calls=%async_computation | async-start | bytes 65536 | tf_op jit(solution)/shard_map/all_to_all | solution.py:243
  27.1 56.4 %collective-permute-start.1 = (f32[1,16,128,128]{3,2,1,0:T(8,128)}, f32[1,16,128,128]{3,2,1,0:T(8,128)}, u32[]{:S(2)}, u32[]{:S(2)}) collective-permute-start(f32[1,16,128,128]{3,2,1,0:T(8,128)} %get-tuple-element.17), channel_id=1, source_target_pairs={{4,0},{8,4},{12,8},{16,12},{20,16},{24,20},{28,24},{32,28},{36,32}... | collective-permute-start | bytes 3145736 | tf_op jit(solution)/shard_map/ppermute | solution.py:236
  32.6 50.9 %collective-permute-start = (f32[1,16,128,128]{3,2,1,0:T(8,128)}, f32[1,16,128,128]{3,2,1,0:T(8,128)}, u32[]{:S(2)}, u32[]{:S(2)}) collective-permute-start(f32[1,16,128,128]{3,2,1,0:T(8,128)} %get-tuple-element.18), channel_id=1, source_target_pairs={{0,4},{4,8},{8,12},{12,16},{16,20},{20,24},{24,28},{28,32},{32,36}... | collective-permute-start | bytes 3145736 | tf_op jit(solution)/shard_map/ppermute | solution.py:235
  42.7 3.3 copy-start.5
  45.9 2.3 copy-start.6
  48.3 2.3 copy-start.7
  60.5 17.8 %all-to-all-start.1 = ((f32[64,1,1]{2,1,0:T(1,128)}), f32[64,1,1]{2,1,0:T(1,128)S(1)}, u32[]{:S(2)}, u32[]{:S(2)}) async-start(f32[64,1,1]{2,1,0:T(1,128)} %broadcast_in_dim.49), calls=%async_computation.1 | async-start | bytes 65536 | tf_op jit(solution)/shard_map/all_to_all | solution.py:243
  125.3 25.5 %collective-permute-start.3 = (f32[1,16,128,128]{3,2,1,0:T(8,128)}, f32[1,16,128,128]{3,2,1,0:T(8,128)}, u32[]{:S(2)}, u32[]{:S(2)}) collective-permute-start(f32[1,16,128,128]{3,2,1,0:T(8,128)} %get-tuple-element.13), channel_id=1, source_target_pairs={{4,0},{8,4},{12,8},{16,12},{20,16},{24,20},{28,24},{32,28},{36,32}... | collective-permute-start | bytes 3145736 | tf_op jit(solution)/shard_map/ppermute | solution.py:236
  126.4 25.7 %collective-permute-start.2 = (f32[1,16,128,128]{3,2,1,0:T(8,128)S(1)}, f32[1,16,128,128]{3,2,1,0:T(8,128)}, u32[]{:S(2)}, u32[]{:S(2)}) collective-permute-start(f32[1,16,128,128]{3,2,1,0:T(8,128)S(1)} %get-tuple-element.14), channel_id=1, source_target_pairs={{0,4},{4,8},{8,12},{12,16},{16,20},{20,24},{24,28},{28,32},{32,36}... | collective-permute-start | bytes 3145736 | tf_op jit(solution)/shard_map/ppermute | solution.py:235
  141.3 3.3 copy-start.13
  144.6 2.3 copy-start.12
  149.3 2.8 copy-start.2
  163.3 3.3 copy-start.15
  189.8 8.4 %copy-start.20 = (s32[128]{0:T(128)S(1)}, s32[128]{0:T(128)}, u32[]{:S(2)}) copy-start(s32[128]{0:T(128)} %param.11) | copy-start | bytes 1540
  189.8 8.4 %copy-start.4 = (f32[2,16,128,128]{3,2,1,0:T(8,128)S(1)}, f32[2,16,128,128]{3,2,1,0:T(8,128)}, u32[]{:S(2)}) copy-start(f32[2,16,128,128]{3,2,1,0:T(8,128)} %get-tuple-element.34) | copy-start | bytes 6291460
  193.1 23.9 %collective-permute-start.5 = (f32[1,16,128,128]{3,2,1,0:T(8,128)}, f32[1,16,128,128]{3,2,1,0:T(8,128)}, u32[]{:S(2)}, u32[]{:S(2)}) collective-permute-start(f32[1,16,128,128]{3,2,1,0:T(8,128)} %get-tuple-element.9), channel_id=1, source_target_pairs={{4,0},{8,4},{12,8},{16,12},{20,16},{24,20},{28,24},{32,28},{36,32}... | collective-permute-start | bytes 3145736 | tf_op jit(solution)/shard_map/ppermute | solution.py:236
  197.9 25.4 %collective-permute-start.4 = (f32[1,16,128,128]{3,2,1,0:T(8,128)}, f32[1,16,128,128]{3,2,1,0:T(8,128)}, u32[]{:S(2)}, u32[]{:S(2)}) collective-permute-start(f32[1,16,128,128]{3,2,1,0:T(8,128)} %get-tuple-element.10), channel_id=1, source_target_pairs={{0,4},{4,8},{8,12},{12,16},{16,20},{20,24},{24,28},{28,32},{32,36}... | collective-permute-start | bytes 3145736 | tf_op jit(solution)/shard_map/ppermute | solution.py:235
  206.3 3.3 copy-start.11
  209.6 2.3 copy-start.10
  234.5 3.4 copy-start.14
  237.9 2.3 copy-start.3
  (5 other events, 8.8 us)

commit v2 on v1

v2 whole, which is shorter than its diff:
```python
import jax
import jax.numpy as jnp
from jax import lax
from jax.experimental import pallas as pl
from jax.experimental.pallas import tpu as pltpu
from jax.sharding import PartitionSpec as P

cut_share = 0.3

MESH = pl.DeviceIdType.MESH
F32 = jnp.float32
BF16 = jnp.bfloat16
exact = lax.Precision.HIGHEST
VMEM_LIMIT = 60 * 1024 * 1024


def place():
    b, st = lax.axis_index("blk"), lax.axis_index("states")
    z = lax.rem(b, 8)
    x = lax.rem(lax.div(b, 8), 4)
    y = lax.div(st, 2) * 2 + lax.div(b, 32)
    return x, y, z, lax.rem(st, 2)


def device(x, y, z, core):
    return ((lax.rem(y, 2) * 4 + x) * 8 + z, lax.div(y, 2) * 2 + core)


def send(src, dst, send_sem, recv_sem, peer):
    copy = pltpu.make_async_remote_copy(
        src_ref=src, dst_ref=dst, send_sem=send_sem, recv_sem=recv_sem, device_id=peer, device_id_type=MESH
    )
    copy.start()
    return copy


def rows_at(start, size):
    return pl.ds(pl.multiple_of(start, 8), size)


def nt(a, b):
    return lax.dot_general(a, b, (((1,), (1,)), ((), ())), preferred_element_type=F32)


def sum_kernel(xt_ref, out_ref, xh_ref, xl_ref, hi, lo, g_ref, r1, a1, r2, a2, r3, zbuf, gbuf, send_sems, recv_sems):
    x, y, z, core = place()
    core_peer = device(x, y, z, 1 - core)
    x_peers = [device(lax.rem(x + d, 4), y, z, core) for d in (1, 2, 3)]
    y_peers = [device(x, lax.rem(y + d, 4), z, core) for d in (1, 2, 3)]
    z_peers = [device(x, y, lax.rem(z + d, 8), core) for d in range(1, 8)]
    peers = [core_peer] + x_peers + y_peers + z_peers
    barrier = pltpu.get_barrier_semaphore()
    for peer in peers:
        pl.semaphore_signal(barrier, inc=1, device_id=peer, device_id_type=MESH)
    for q in range(8):
        cols = slice(128 * q, 128 * q + 128)
        hi[:, cols], lo[:, cols] = halves(xt_ref[q])
    for i in range(4):
        here, upto = slice(128 * i, 128 * i + 128), 128 * i + 128
        block = nt(hi[here], hi[:upto]) + (nt(hi[here], lo[:upto]) + nt(lo[here], hi[:upto]))
        for j in range(i + 1):
            g_ref[128 * SLOT[i, j] : 128 * SLOT[i, j] + 128] = block[:, 128 * j : 128 * j + 128]
    pl.semaphore_wait(barrier, len(peers))
    used = iter(range(21))

    def sems():
        i = next(used)
        return send_sems.at[i], recv_sems.at[i]

    copy = send(g_ref.at[rows_at((1 - core) * 640, 640)], r1, *sems(), core_peer)
    copy.wait()
    a1[...] = g_ref[rows_at(core * 640, 640)] + r1[...]
    copies = [
        send(a1.at[rows_at(lax.rem(x + d, 4) * 160, 160)], r2.at[d - 1], *sems(), x_peers[d - 1]) for d in (1, 2, 3)
    ]

    @pl.loop(0, 8)
    def _(q):
        at = pl.ds(pl.multiple_of((lax.rem(q, 2) * 4 + lax.div(q, 2)) * 128, 128), 128)
        for d in range(4):
            cols = slice(128 * d, 128 * d + 128)
            xh_ref[at, cols], xl_ref[at, cols] = halves(xt_ref[q, cols].T)

    for copy in copies:
        copy.wait()
    a2[...] = (a1[rows_at(x * 160, 160)] + r2[0]) + (r2[1] + r2[2])
    copies = [
        send(a2.at[rows_at(lax.rem(y + d, 4) * 40, 40)], r3.at[d - 1], *sems(), y_peers[d - 1]) for d in (1, 2, 3)
    ]
    for copy in copies:
        copy.wait()
    zbuf[z] = (a2[rows_at(y * 40, 40)] + r3[0]) + (r3[1] + r3[2])
    copies = [send(zbuf.at[z], zbuf.at[z], *sems(), z_peers[d - 1]) for d in range(1, 8)]
    for copy in copies:
        copy.wait()
    own = rows_at(core * 640 + x * 160 + y * 40, 40)
    gbuf[own] = ((zbuf[0] + zbuf[1]) + (zbuf[2] + zbuf[3])) + ((zbuf[4] + zbuf[5]) + (zbuf[6] + zbuf[7]))
    copies = [send(gbuf.at[own], gbuf.at[own], *sems(), peer) for peer in y_peers]
    for copy in copies:
        copy.wait()
    own = rows_at(core * 640 + x * 160, 160)
    copies = [send(gbuf.at[own], gbuf.at[own], *sems(), peer) for peer in x_peers]
    for copy in copies:
        copy.wait()
    own = rows_at(core * 640, 640)
    send(gbuf.at[own], gbuf.at[own], *sems(), core_peer).wait()
    out_ref[...] = gbuf[...]


def gram_over_devices(xt):
    vmem = pl.BlockSpec(memory_space=pltpu.VMEM)
    return pl.pallas_call(
        sum_kernel,
        out_shape=[
            jax.ShapeDtypeStruct((1280, 128), F32),
            jax.ShapeDtypeStruct((1024, 512), BF16),
            jax.ShapeDtypeStruct((1024, 512), BF16),
        ],
        in_specs=[vmem],
        out_specs=[vmem] * 3,
        scratch_shapes=[
            pltpu.VMEM((512, 1024), BF16),
            pltpu.VMEM((512, 1024), BF16),
            pltpu.VMEM((1280, 128), F32),
            pltpu.VMEM((640, 128), F32),
            pltpu.VMEM((640, 128), F32),
            pltpu.VMEM((3, 160, 128), F32),
            pltpu.VMEM((160, 128), F32),
            pltpu.VMEM((3, 40, 128), F32),
            pltpu.VMEM((8, 40, 128), F32),
            pltpu.VMEM((1280, 128), F32),
            pltpu.SemaphoreType.DMA((21,)),
            pltpu.SemaphoreType.DMA((21,)),
        ],
        compiler_params=pltpu.CompilerParams(collective_id=1, has_side_effects=True, vmem_limit_bytes=VMEM_LIMIT),
        name="gram_sum",
    )(xt.reshape(8, 512, 128))


PAIRS = [(i, j) for i in range(4) for j in range(i + 1)]
SLOT = {pair: n for n, pair in enumerate(PAIRS)}


def halves(v):
    hi = v.astype(BF16)
    return hi, (v - hi.astype(F32)).astype(BF16)


def thirds(v):
    hi = v.astype(BF16).astype(F32)
    rest = v - hi
    mid = rest.astype(BF16).astype(F32)
    return hi, mid, rest - mid


def dot_nt(a, b):
    return lax.dot_general(a, b, (((1,), (1,)), ((), ())), precision=exact, preferred_element_type=F32)


def dot_nn(a, b):
    return lax.dot_general(a, b, (((1,), (0,)), ((), ())), precision=exact, preferred_element_type=F32)


def eliminate(work):
    row = lax.broadcasted_iota(jnp.int32, (8, 128), 0)
    for p in range(16):
        lo = 8 * p
        left, right = work[lo : lo + 8, :128], work[lo : lo + 8, 128:]
        cols = [jnp.broadcast_to(left[:, lo + c : lo + c + 1], (8, 128)) for c in range(8)]
        for j in range(8):
            scale = lax.rsqrt(jnp.broadcast_to(cols[j][j : j + 1, :], (8, 128)))
            lrow = jnp.broadcast_to(left[j : j + 1, :], (8, 128)) * scale
            rrow = jnp.broadcast_to(right[j : j + 1, :], (8, 128)) * scale
            factor = jnp.where(row > j, cols[j] * scale, 0.0)
            for c in range(j + 1, 8):
                cols[c] = cols[c] - factor * (jnp.broadcast_to(cols[c][j : j + 1, :], (8, 128)) * scale)
            left = jnp.where(row == j, lrow, left - factor * lrow)
            right = jnp.where(row == j, rrow, right - factor * rrow)
        work[lo : lo + 8, :128] = left
        work[lo : lo + 8, 128:] = right
        if p < 15:
            h, m, l = thirds(jnp.concatenate([left, right], axis=1))
            lhs = jnp.concatenate([h[:, :128], h[:, :128], m[:, :128], m[:, :128], h[:, :128], l[:, :128]], axis=0).astype(BF16)
            rhs = jnp.concatenate([h, m, h, m, l, h], axis=0).astype(BF16)
            change = lax.dot_general(lhs, rhs, (((0,), (0,)), ((), ())), preferred_element_type=F32)
            work[lo + 8 :, :] = work[lo + 8 :, :] - change[lo + 8 :, :]


def factor_kernel(g_ref, xh, xl, out_ref, blocks, work, low, inv, ih, il):
    blocks[...] = g_ref[...]
    inv[...] = jnp.zeros_like(inv)
    eye = (lax.broadcasted_iota(jnp.int32, (128, 128), 0) == lax.broadcasted_iota(jnp.int32, (128, 128), 1)).astype(F32)

    @pl.loop(0, 4)
    def _(k):
        work[:, :128] = blocks[lax.div(k * (k + 1), 2) + k]
        work[:, 128:] = eye
        eliminate(work)
        for n in range(4):

            @pl.when(k == n)
            def _():
                here = slice(128 * n, 128 * n + 128)
                w = work[:, 128:]
                inv[here, here] = w
                if n > 0:
                    known = dot_nn(low[here, : 128 * n], inv[: 128 * n, : 128 * n])
                    inv[here, : 128 * n] = -dot_nn(w, known)
                for i in range(n + 1, 4):
                    low[128 * i : 128 * i + 128, here] = dot_nt(blocks[SLOT[i, n]], w)
                for j in range(n + 1, 4):
                    for i in range(j, 4):
                        blocks[SLOT[i, j]] = blocks[SLOT[i, j]] - dot_nt(
                            low[128 * i : 128 * i + 128, here], low[128 * j : 128 * j + 128, here]
                        )

    ih[...], il[...] = halves(inv[...])

    for i in range(4):
        here, upto = slice(128 * i, 128 * i + 128), 128 * i + 128
        a, b = xh[:, :upto], xl[:, :upto]
        u, v = ih[here, :upto], il[here, :upto]
        out_ref[:, here] = nt(a, u) + (nt(a, v) + nt(b, u))


def orthonormalised(packed, xh, xl):
    vmem = pl.BlockSpec(memory_space=pltpu.VMEM)
    return pl.pallas_call(
        factor_kernel,
        out_shape=jax.ShapeDtypeStruct((1024, 512), F32),
        in_specs=[vmem] * 3,
        out_specs=vmem,
        scratch_shapes=[
            pltpu.VMEM((10, 128, 128), F32),
            pltpu.VMEM((128, 256), F32),
            pltpu.VMEM((512, 512), F32),
            pltpu.VMEM((512, 512), F32),
            pltpu.VMEM((512, 512), BF16),
            pltpu.VMEM((512, 512), BF16),
        ],
        compiler_params=pltpu.CompilerParams(vmem_limit_bytes=VMEM_LIMIT),
        name="factor",
    )(packed.reshape(10, 128, 128), xh, xl)


NCH = 2
WIDTH = 128 // NCH


def both_halves(v):
    hi, lo = halves(v)
    return jnp.concatenate([hi, lo], axis=0)


def product(lhs, rhs):
    full = lax.dot_general(lhs, rhs, (((1,), (0,)), ((), ())), preferred_element_type=F32)
    return (full[:WIDTH, :128] + full[WIDTH:, :128]) + (full[:WIDTH, 128:] + full[WIDTH:, 128:])


def filter_kernel(index_ref, offset_ref, start_ref, coup_ref, pot_ref, deg_ref, xt_ref, *scratch):
    scratch = iter(scratch)
    field = [[next(scratch) for _ in range(NCH)] for _ in range(3)]
    stack = [[next(scratch) for _ in range(NCH)] for _ in range(3)]
    halo = [[[next(scratch) for _ in range(2)] for _ in range(NCH)] for _ in range(3)]
    partial = next(scratch)
    chosen = [next(scratch) for _ in range(NCH)]
    blocks, row_abs, diag = next(scratch), next(scratch), next(scratch)
    zb, xb, yb = next(scratch), next(scratch), next(scratch)
    degree = next(scratch)
    send_sems, recv_sems = next(scratch), next(scratch)
    used = iter(range(12 * NCH + 11))

    def sems():
        i = next(used)
        return send_sems.at[i], recv_sems.at[i]

    b, st = lax.axis_index("blk"), lax.axis_index("states")
    z, xx, ylo = lax.rem(b, 8), lax.rem(lax.div(b, 8), 4), lax.div(b, 32)
    left, right = (lax.rem(b + 63, 64), st), (lax.rem(b + 1, 64), st)
    z_peers = [(b - z + lax.rem(z + d, 8), st) for d in range(1, 8)]
    x_peers = [(b - xx * 8 + lax.rem(xx + d, 4) * 8, st) for d in range(1, 4)]
    y_peer = (lax.rem(b + 32, 64), st)
    state_peers = [(b, lax.rem(st + d, 4)) for d in range(1, 4)]
    peers = [left, right, y_peer] + z_peers + x_peers + state_peers
    barrier = pltpu.get_barrier_semaphore()
    for peer in peers:
        pl.semaphore_signal(barrier, inc=1, device_id=peer, device_id_type=MESH)

    @pl.loop(0, 16)
    def _(s):
        for l in range(2):
            turned = start_ref[l, s].T
            for c in range(NCH):
                part = turned[WIDTH * c : WIDTH * c + WIDTH]
                field[0][c][l, s] = part
                stack[0][c][l, s] = both_halves(part)

    pl.semaphore_wait(barrier, len(peers))
    copies = []
    edge = {}

    def send_edge(k, c, l):
        source = field[k][c].at[l]
        copy = send(source, halo[k][c][1 - l], *sems(), right if l else left)
        copies.append(copy)
        edge[k, c, 1 - l] = copy

    for c in range(NCH):
        send_edge(0, c, 0)
        send_edge(0, c, 1)

    eye = lax.broadcasted_iota(jnp.int32, (128, 128), 0) == lax.broadcasted_iota(jnp.int32, (128, 128), 1)

    @pl.loop(0, 16)
    def _(n):
        turned = coup_ref[n].T
        row_abs[pl.ds(n, 1)] = jnp.sum(jnp.abs(turned), axis=0, keepdims=True)
        diag[pl.ds(n, 1)] = jnp.sum(jnp.where(eye, turned, 0.0), axis=0, keepdims=True)
        blocks[n] = jnp.concatenate(halves(turned), axis=1)

    def bounds_of(s, ends):
        top, low = ends
        for l in range(2):
            first = index_ref[l, 0, s]
            middle = diag[pl.ds(first, 1)]
            center = middle + pot_ref[l, pl.ds(s, 1)]
            radius = row_abs[pl.ds(first, 1)] - jnp.abs(middle)
            rest = row_abs[pl.ds(index_ref[l, 1, s], 1)]
            for slot in range(2, 7):
                rest = rest + row_abs[pl.ds(index_ref[l, slot, s], 1)]
            radius = radius + rest
            top = jnp.maximum(top, center + radius)
            low = jnp.maximum(low, radius - center)
        return top, low

    least = jnp.full((1, 128), -3e38, F32)
    top, low = lax.fori_loop(0, 16, bounds_of, (least, least))
    zb[z] = jnp.concatenate([jnp.broadcast_to(top, (8, 128)), jnp.broadcast_to(low, (8, 128))], axis=0)

    def exchange(buf, at, group):
        started = [send(buf.at[at], buf.at[at], *sems(), peer) for peer in group]
        copies.extend(started)
        return started

    def merged(buf, started):
        for copy in started:
            copy.wait_recv()
        best = buf[0]
        for i in range(1, buf.shape[0]):
            best = jnp.maximum(best, buf[i])
        return best

    def local_part(k, c):
        @pl.loop(0, 16)
        def _(s):
            for l in range(2):
                sources = [(l, s)]
                for slot in range(1, 5):
                    sources.append((l, (s + offset_ref[l, slot - 1, s]) & 15))
                slots = [0, 1, 2, 3, 4, 6 - l]
                sources.append((1 - l, (s + offset_ref[l, 5 - l, s]) & 15))
                lhs = jnp.concatenate([stack[k][c][at] for at in sources], axis=1)
                rhs = jnp.concatenate([blocks[index_ref[l, slot, s]] for slot in slots], axis=0)
                partial[l, s] = product(lhs, rhs)

    def finish(k, c, middle, inverse):
        for l in range(2):
            edge[k, c, l].wait_recv()

            @pl.loop(0, 16)
            def _(s):
                slot = 5 + l
                outer = halo[k][c][l][(s + offset_ref[l, slot - 1, s]) & 15]
                total = partial[l, s] + product(both_halves(outer), blocks[index_ref[l, slot, s]])
                own = field[k][c][l, s]
                new = (total + (pot_ref[l, pl.ds(s, 1)] - middle) * own) * inverse
                if k > 0:
                    new = 2.0 * new - field[k - 1][c][l, s]
                if k < 2:
                    field[k + 1][c][l, s] = new
                    stack[k + 1][c][l, s] = both_halves(new)
                else:
                    d = degree[WIDTH * c : WIDTH * c + WIDTH]
                    chosen[c][s, l] = jnp.where(d == 1, field[1][c][l, s], jnp.where(d == 2, own, new))

            if k < 2:
                send_edge(k + 1, c, l)

    started = exchange(zb, z, z_peers)
    degree[...] = jnp.broadcast_to(deg_ref[...].astype(F32), (128, 128)).T.astype(jnp.int32)
    local_part(0, 0)
    xb[xx] = merged(zb, started)
    started = exchange(xb, xx, x_peers)
    best = merged(xb, started)
    yb[ylo] = best
    started = exchange(yb, ylo, [y_peer])
    best = merged(yb, started)
    upper = jnp.max(best[:8], axis=1, keepdims=True)[:1]
    lower = -jnp.max(best[8:], axis=1, keepdims=True)[:1]
    cut_edge = lower + cut_share * (upper - lower)
    middle = jnp.broadcast_to((upper + cut_edge) / 2.0, (1, 128))
    inverse = jnp.broadcast_to(2.0 / (upper - cut_edge), (1, 128))

    arrivals = []
    for k in range(3):
        for c in range(NCH):
            if (k, c) != (0, 0):
                local_part(k, c)
            finish(k, c, middle, inverse)
            if k == 2:
                rows = pl.ds(pl.multiple_of(128 * st + WIDTH * c, WIDTH), WIDTH)
                for d in (1, 2, 3):
                    other = lax.rem(st + d, 4)
                    copy = send(
                        chosen[c].at[pl.ds(4 * other, 4)], xt_ref.at[:, :, rows], *sems(), state_peers[d - 1]
                    )
                    copies.append(copy)
                    arrivals.append(copy)
                for s in range(4):
                    for l in range(2):
                        xt_ref[s, l, rows] = chosen[c][4 * st + s, l]
    for copy in arrivals:
        copy.wait_recv()
    for copy in copies:
        copy.wait_send()


def filtered_rows(start_states, couplings, potential, site_offsets, coupling_index, degrees):
    vmem, smem = pl.BlockSpec(memory_space=pltpu.VMEM), pl.BlockSpec(memory_space=pltpu.SMEM)
    scratch = [pltpu.VMEM((2, 16, WIDTH, 128), F32)] * (3 * NCH)
    scratch += [pltpu.VMEM((2, 16, 2 * WIDTH, 128), BF16)] * (3 * NCH)
    scratch += [pltpu.VMEM((16, WIDTH, 128), F32)] * (6 * NCH)
    scratch += [pltpu.VMEM((2, 16, WIDTH, 128), F32)]
    scratch += [pltpu.VMEM((16, 2, WIDTH, 128), F32)] * NCH
    scratch += [pltpu.VMEM((16, 128, 256), BF16), pltpu.VMEM((16, 128), F32), pltpu.VMEM((16, 128), F32)]
    scratch += [pltpu.VMEM((n, 16, 128), F32) for n in (8, 4, 2)]
    scratch += [pltpu.VMEM((128, 128), jnp.int32)]
    scratch += [pltpu.SemaphoreType.DMA((12 * NCH + 11,))] * 2
    return pl.pallas_call(
        filter_kernel,
        out_shape=jax.ShapeDtypeStruct((4, 2, 512, 128), F32),
        in_specs=[smem, smem, vmem, vmem, vmem, vmem],
        out_specs=vmem,
        scratch_shapes=scratch,
        compiler_params=pltpu.CompilerParams(collective_id=0, has_side_effects=True, vmem_limit_bytes=VMEM_LIMIT),
        name="filter",
    )(coupling_index, site_offsets, start_states, couplings, potential, degrees.reshape(1, 128))


def per_device(start_states, couplings, potential, site_offsets, coupling_index, degrees):
    xt = filtered_rows(start_states, couplings, potential, site_offsets, coupling_index, degrees)
    gram, xh, xl = gram_over_devices(xt)
    return orthonormalised(gram, xh, xl).reshape(2, 4, 128, 512)


def solution(mesh):
    in_specs = (
        P("blk", None, None, "states"),
        P(),
        P("blk", None, None),
        P("blk", None, None),
        P("blk", None, None),
        P("states"),
    )
    out_specs = P("blk", "states", None, None)
    return jax.shard_map(
        per_device, mesh=mesh, in_specs=in_specs, out_specs=out_specs, check_vma=False
    )
```

time: 381 us -> 192 us (0.50); the launches traced: 374 us -> 191 us
  local copies, waits for them, and re-layouts: 133 us -> 2.58 us
  Pallas kernels: 67.7 us -> 189 us
  matrix products: 68.9 us -> 0 us
  blocking collectives: 35.3 us -> 0 us
  starting transfers between devices: 34.2 us -> 0 us
  waiting for transfers between devices: 16.6 us -> 0 us
  other arithmetic: 14.9 us -> 0 us
    pallas_call x1 -> x2, Pallas kernels: 34.2 us -> 156 us  [the longest x1 121 us: filtered_rows(): pl.pallas_call(filter_kernel, out_shape=jax.ShapeDtypeStruct((4, 2, 512,...]
    dot_general x6 -> x0, matrix products: 68.9 us -> none  [the longest x3 64.3 us: apply_inner(): jnp.einsum('lksij,lksjn->lsin', blocks_used, stacked, precision=exact)]
    gather x20 -> x0, local copies, waits for them, and re-layouts: 60.6 us -> none  [the longest x18 52.1 us: apply_inner(): pieces.append(source[layer_ids[:, None], neighbour])]
    unnamed x68 -> x2, local copies, waits for them, and re-layouts: 49.4 us -> 2.58 us
    all_to_all x1 -> x0, blocking collectives: 35.3 us -> none  [per_device(): lax.all_to_all(chosen, 'states', split_axis=1, concat_axis=3, tiled=True)]
    all_to_all x2 -> x0, starting transfers between devices: 21.9 us -> none  [copy_for_each(): return lax.all_to_all(copies, axis, split_axis=0, concat_axis=0, tiled=True)]
    ppermute x6 -> x0, starting transfers between devices: 12.2 us -> none  [the longest x3 11.5 us: padded_2(): after = lax.ppermute(first, axis, down)]
    concatenate x5 -> x0, other arithmetic: 12 us -> none  [the longest x3 12 us: padded_2(): shard = jnp.concatenate([before, shard, after], axis=dim)]
  transfers between devices with their start and end apart: 8 -> 0, of which waited for: 4 -> 0; matrix products, arithmetic and copies ran while one was open for 19% -> 0% of each run, Pallas kernels for 0% -> 0%
where the time goes in v2:
time: 192 us; the launch traced here: 191 us
  Pallas kernels  189 us (98%)
  local copies, waits for them, and re-layouts  2.58 us (1%)
    pallas_call x1, Pallas kernels, filtered_rows(): pl.pallas_call(filter_kernel, out_shape=jax.ShapeDtypeStruct((4, 2, 512,...  121 us
    pallas_call x1, Pallas kernels, gram_over_devices(): pl.pallas_call(sum_kernel, out_shape=[jax.ShapeDtypeStruct((1280, 128), F...  34.2 us
    pallas_call x1, Pallas kernels, orthonormalised(): pl.pallas_call(factor_kernel, out_shape=jax.ShapeDtypeStruct((1024, 512),...  33.1 us

profile of v2, /device:TPU:1, one launch (start us, length us, event | category | flops | bytes accessed | tf_op | source)
XLA Modules:
  0.0 191.5 jit_solution(11384236888103680599)
XLA Ops:
  0.0 1.3 copy.8.offset_ref
  1.3 1.3 copy.7.index_ref
  2.6 121.5 %filter.1 = f32[4,2,512,128]{3,2,1,0:T(8,128)} custom-call(s32[2,7,16]{2,1,0:T(8,128)} %copy.7.index_ref, s32[2,6,16]{2,1,0:T(8,128)} %copy.8.offset_ref, f32[2,16,128,128]{3,2,1,0:T(8,128)} %start_ref.1, f32[16,128,128]{2,1,0:T(8,128)} %coup_ref.1, f32[2,16,128]{2,1,0:T(8,128)} %pot_ref.1, s32[1,128]{1,0:T(1,128)} %bitcast.6), custom_call_target="tpu_custom_call" | custom-call | tf_op jit(solution)/shard_map/filter/pallas_call | solution.py:439
  124.1 34.2 %gram_sum.1 = (f32[1280,128]{1,0:T(8,128)}, bf16[1024,512]{1,0:T(8,128)(2,1)}, bf16[1024,512]{1,0:T(8,128)(2,1)}) custom-call(f32[8,512,128]{2,1,0:T(8,128)} %bitcast.4), custom_call_target="tpu_custom_call" | custom-call | tf_op jit(solution)/shard_map/gram_sum/pallas_call | solution.py:112
  158.3 33.1 %factor.1 = f32[1024,512]{1,0:T(8,128)} custom-call(f32[10,128,128]{2,1,0:T(8,128)} %bitcast.5, bf16[1024,512]{1,0:T(8,128)(2,1)} %get-tuple-element.9.xh, bf16[1024,512]{1,0:T(8,128)(2,1)} %get-tuple-element.10.xl), custom_call_target="tpu_custom_call" | custom-call | tf_op jit(solution)/shard_map/factor/pallas_call | solution.py:228

commit v3 on v2

--- a/solution.py
+++ b/solution.py
@@ -42,101 +42,6 @@
     return lax.dot_general(a, b, (((1,), (1,)), ((), ())), preferred_element_type=F32)
 
 
-def sum_kernel(xt_ref, out_ref, xh_ref, xl_ref, hi, lo, g_ref, r1, a1, r2, a2, r3, zbuf, gbuf, send_sems, recv_sems):
-    x, y, z, core = place()
-    core_peer = device(x, y, z, 1 - core)
-    x_peers = [device(lax.rem(x + d, 4), y, z, core) for d in (1, 2, 3)]
-    y_peers = [device(x, lax.rem(y + d, 4), z, core) for d in (1, 2, 3)]
-    z_peers = [device(x, y, lax.rem(z + d, 8), core) for d in range(1, 8)]
-    peers = [core_peer] + x_peers + y_peers + z_peers
-    barrier = pltpu.get_barrier_semaphore()
-    for peer in peers:
-        pl.semaphore_signal(barrier, inc=1, device_id=peer, device_id_type=MESH)
-    for q in range(8):
-        cols = slice(128 * q, 128 * q + 128)
-        hi[:, cols], lo[:, cols] = halves(xt_ref[q])
-    for i in range(4):
-        here, upto = slice(128 * i, 128 * i + 128), 128 * i + 128
-        block = nt(hi[here], hi[:upto]) + (nt(hi[here], lo[:upto]) + nt(lo[here], hi[:upto]))
-        for j in range(i + 1):
-            g_ref[128 * SLOT[i, j] : 128 * SLOT[i, j] + 128] = block[:, 128 * j : 128 * j + 128]
-    pl.semaphore_wait(barrier, len(peers))
-    used = iter(range(21))
-
-    def sems():
-        i = next(used)
-        return send_sems.at[i], recv_sems.at[i]
-
-    copy = send(g_ref.at[rows_at((1 - core) * 640, 640)], r1, *sems(), core_peer)
-    copy.wait()
-    a1[...] = g_ref[rows_at(core * 640, 640)] + r1[...]
-    copies = [
-        send(a1.at[rows_at(lax.rem(x + d, 4) * 160, 160)], r2.at[d - 1], *sems(), x_peers[d - 1]) for d in (1, 2, 3)
-    ]
-
-    @pl.loop(0, 8)
-    def _(q):
-        at = pl.ds(pl.multiple_of((lax.rem(q, 2) * 4 + lax.div(q, 2)) * 128, 128), 128)
-        for d in range(4):
-            cols = slice(128 * d, 128 * d + 128)
-            xh_ref[at, cols], xl_ref[at, cols] = halves(xt_ref[q, cols].T)
-
-    for copy in copies:
-        copy.wait()
-    a2[...] = (a1[rows_at(x * 160, 160)] + r2[0]) + (r2[1] + r2[2])
-    copies = [
-        send(a2.at[rows_at(lax.rem(y + d, 4) * 40, 40)], r3.at[d - 1], *sems(), y_peers[d - 1]) for d in (1, 2, 3)
-    ]
-    for copy in copies:
-        copy.wait()
-    zbuf[z] = (a2[rows_at(y * 40, 40)] + r3[0]) + (r3[1] + r3[2])
-    copies = [send(zbuf.at[z], zbuf.at[z], *sems(), z_peers[d - 1]) for d in range(1, 8)]
-    for copy in copies:
-        copy.wait()
-    own = rows_at(core * 640 + x * 160 + y * 40, 40)
-    gbuf[own] = ((zbuf[0] + zbuf[1]) + (zbuf[2] + zbuf[3])) + ((zbuf[4] + zbuf[5]) + (zbuf[6] + zbuf[7]))
-    copies = [send(gbuf.at[own], gbuf.at[own], *sems(), peer) for peer in y_peers]
-    for copy in copies:
-        copy.wait()
-    own = rows_at(core * 640 + x * 160, 160)
-    copies = [send(gbuf.at[own], gbuf.at[own], *sems(), peer) for peer in x_peers]
-    for copy in copies:
-        copy.wait()
-    own = rows_at(core * 640, 640)
-    send(gbuf.at[own], gbuf.at[own], *sems(), core_peer).wait()
-    out_ref[...] = gbuf[...]
-
-
-def gram_over_devices(xt):
-    vmem = pl.BlockSpec(memory_space=pltpu.VMEM)
-    return pl.pallas_call(
-        sum_kernel,
-        out_shape=[
-            jax.ShapeDtypeStruct((1280, 128), F32),
-            jax.ShapeDtypeStruct((1024, 512), BF16),
-            jax.ShapeDtypeStruct((1024, 512), BF16),
-        ],
-        in_specs=[vmem],
-        out_specs=[vmem] * 3,
-        scratch_shapes=[
-            pltpu.VMEM((512, 1024), BF16),
-            pltpu.VMEM((512, 1024), BF16),
-            pltpu.VMEM((1280, 128), F32),
-            pltpu.VMEM((640, 128), F32),
-            pltpu.VMEM((640, 128), F32),
-            pltpu.VMEM((3, 160, 128), F32),
-            pltpu.VMEM((160, 128), F32),
-            pltpu.VMEM((3, 40, 128), F32),
-            pltpu.VMEM((8, 40, 128), F32),
-            pltpu.VMEM((1280, 128), F32),
-            pltpu.SemaphoreType.DMA((21,)),
-            pltpu.SemaphoreType.DMA((21,)),
-        ],
-        compiler_params=pltpu.CompilerParams(collective_id=1, has_side_effects=True, vmem_limit_bytes=VMEM_LIMIT),
-        name="gram_sum",
-    )(xt.reshape(8, 512, 128))
-
-
 PAIRS = [(i, j) for i in range(4) for j in range(i + 1)]
 SLOT = {pair: n for n, pair in enumerate(PAIRS)}
 
@@ -154,36 +59,70 @@
 
 
 def dot_nt(a, b):
-    return lax.dot_general(a, b, (((1,), (1,)), ((), ())), precision=exact, preferred_element_type=F32)
+    h, m, l = thirds(a)
+    u, v, w = thirds(b)
+    lhs = jnp.concatenate([h, h, m, m, h, l], axis=1).astype(BF16)
+    rhs = jnp.concatenate([u, v, u, v, w, u], axis=1).astype(BF16)
+    return lax.dot_general(lhs, rhs, (((1,), (1,)), ((), ())), preferred_element_type=F32)
 
 
 def dot_nn(a, b):
-    return lax.dot_general(a, b, (((1,), (0,)), ((), ())), precision=exact, preferred_element_type=F32)
+    h, m, l = thirds(a)
+    u, v, w = thirds(b)
+    lhs = jnp.concatenate([h, h, m, m, h, l], axis=1).astype(BF16)
+    rhs = jnp.concatenate([u, v, u, v, w, u], axis=0).astype(BF16)
+    return lax.dot_general(lhs, rhs, (((1,), (0,)), ((), ())), preferred_element_type=F32)
 
 
 def eliminate(work):
-    row = lax.broadcasted_iota(jnp.int32, (8, 128), 0)
-    for p in range(16):
-        lo = 8 * p
-        left, right = work[lo : lo + 8, :128], work[lo : lo + 8, 128:]
-        cols = [jnp.broadcast_to(left[:, lo + c : lo + c + 1], (8, 128)) for c in range(8)]
-        for j in range(8):
+    row = lax.broadcasted_iota(jnp.int32, (16, 128), 0)
+
+    def spread(v, rows=16):
+        return jnp.broadcast_to(v, (rows, 128))
+
+    def steps(lo, count):
+        left, right = work[lo : lo + 16, :128], work[lo : lo + 16, 128:]
+        cols = [spread(left[:, lo + c : lo + c + 1]) for c in range(16)]
+        below = []
+        for t in range(1, count):
+            l2, r2 = work[lo + 16 * t : lo + 16 * t + 16, :128], work[lo + 16 * t : lo + 16 * t + 16, 128:]
+            below.append([l2, r2, [spread(l2[:, lo + c : lo + c + 1]) for c in range(16)]])
+        for j in range(16):
             scale = lax.rsqrt(jnp.broadcast_to(cols[j][j : j + 1, :], (8, 128)))
-            lrow = jnp.broadcast_to(left[j : j + 1, :], (8, 128)) * scale
-            rrow = jnp.broadcast_to(right[j : j + 1, :], (8, 128)) * scale
+            scale = jnp.concatenate([scale] * 2, axis=0)
             factor = jnp.where(row > j, cols[j] * scale, 0.0)
-            for c in range(j + 1, 8):
-                cols[c] = cols[c] - factor * (jnp.broadcast_to(cols[c][j : j + 1, :], (8, 128)) * scale)
+            lrow = spread(left[j : j + 1, :]) * scale
+            rrow = spread(right[j : j + 1, :]) * scale
+            lower = [part[2][j] * scale for part in below]
+            for c in range(j + 1, 16):
+                across = spread(cols[c][j : j + 1, :]) * scale
+                cols[c] = cols[c] - factor * across
+                for part, f in zip(below, lower):
+                    part[2][c] = part[2][c] - f * across
             left = jnp.where(row == j, lrow, left - factor * lrow)
             right = jnp.where(row == j, rrow, right - factor * rrow)
-        work[lo : lo + 8, :128] = left
-        work[lo : lo + 8, 128:] = right
-        if p < 15:
-            h, m, l = thirds(jnp.concatenate([left, right], axis=1))
+            for part, f in zip(below, lower):
+                part[0] = part[0] - f * lrow
+                part[1] = part[1] - f * rrow
+        work[lo : lo + 16, :128] = left
+        work[lo : lo + 16, 128:] = right
+        for t in range(1, count):
+            work[lo + 16 * t : lo + 16 * t + 16, :128] = below[t - 1][0]
+            work[lo + 16 * t : lo + 16 * t + 16, 128:] = below[t - 1][1]
+
+    for p in range(128 // PANEL):
+        lo = PANEL * p
+        for t in range(PANEL // 16):
+            steps(lo + 16 * t, PANEL // 16 - t)
+        if lo + PANEL < 128:
+            h, m, l = thirds(work[lo : lo + PANEL, :])
             lhs = jnp.concatenate([h[:, :128], h[:, :128], m[:, :128], m[:, :128], h[:, :128], l[:, :128]], axis=0).astype(BF16)
             rhs = jnp.concatenate([h, m, h, m, l, h], axis=0).astype(BF16)
             change = lax.dot_general(lhs, rhs, (((0,), (0,)), ((), ())), preferred_element_type=F32)
-            work[lo + 8 :, :] = work[lo + 8 :, :] - change[lo + 8 :, :]
+            work[lo + PANEL :, :] = work[lo + PANEL :, :] - change[lo + PANEL :, :]
+
+
+PANEL = 32
 
 
 def factor_kernel(g_ref, xh, xl, out_ref, blocks, work, low, inv, ih, il):
@@ -245,6 +184,7 @@
 
 NCH = 2
 WIDTH = 128 // NCH
+COPIES = 6 * NCH + 3 * NCH + 9 + 11 + 33
 
 
 def both_halves(v):
@@ -257,7 +197,7 @@
     return (full[:WIDTH, :128] + full[WIDTH:, :128]) + (full[:WIDTH, 128:] + full[WIDTH:, 128:])
 
 
-def filter_kernel(index_ref, offset_ref, start_ref, coup_ref, pot_ref, deg_ref, xt_ref, *scratch):
+def filter_kernel(index_ref, offset_ref, start_ref, coup_ref, pot_ref, deg_ref, gram_ref, xh_ref, xl_ref, *scratch):
     scratch = iter(scratch)
     field = [[next(scratch) for _ in range(NCH)] for _ in range(3)]
     stack = [[next(scratch) for _ in range(NCH)] for _ in range(3)]
@@ -267,8 +207,10 @@
     blocks, row_abs, diag = next(scratch), next(scratch), next(scratch)
     zb, xb, yb = next(scratch), next(scratch), next(scratch)
     degree = next(scratch)
+    xt_ref = next(scratch)
+    sums = [next(scratch) for _ in range(10)]
     send_sems, recv_sems = next(scratch), next(scratch)
-    used = iter(range(12 * NCH + 11))
+    used = iter(range(COPIES))
 
     def sems():
         i = next(used)
@@ -281,7 +223,8 @@
     x_peers = [(b - xx * 8 + lax.rem(xx + d, 4) * 8, st) for d in range(1, 4)]
     y_peer = (lax.rem(b + 32, 64), st)
     state_peers = [(b, lax.rem(st + d, 4)) for d in range(1, 4)]
-    peers = [left, right, y_peer] + z_peers + x_peers + state_peers
+    sum_peers = partners()
+    peers = [left, right, y_peer] + z_peers + x_peers + state_peers + [peer for group in sum_peers for peer in group]
     barrier = pltpu.get_barrier_semaphore()
     for peer in peers:
         pl.semaphore_signal(barrier, inc=1, device_id=peer, device_id_type=MESH)
@@ -321,13 +264,13 @@
     def bounds_of(s, ends):
         top, low = ends
         for l in range(2):
-            first = index_ref[l, 0, s]
+            first = index_ref[0, l, s]
             middle = diag[pl.ds(first, 1)]
             center = middle + pot_ref[l, pl.ds(s, 1)]
             radius = row_abs[pl.ds(first, 1)] - jnp.abs(middle)
-            rest = row_abs[pl.ds(index_ref[l, 1, s], 1)]
+            rest = row_abs[pl.ds(index_ref[1, l, s], 1)]
             for slot in range(2, 7):
-                rest = rest + row_abs[pl.ds(index_ref[l, slot, s], 1)]
+                rest = rest + row_abs[pl.ds(index_ref[slot, l, s], 1)]
             radius = radius + rest
             top = jnp.maximum(top, center + radius)
             low = jnp.maximum(low, radius - center)
@@ -356,11 +299,11 @@
             for l in range(2):
                 sources = [(l, s)]
                 for slot in range(1, 5):
-                    sources.append((l, (s + offset_ref[l, slot - 1, s]) & 15))
+                    sources.append((l, (s + offset_ref[slot - 1, l, s]) & 15))
                 slots = [0, 1, 2, 3, 4, 6 - l]
-                sources.append((1 - l, (s + offset_ref[l, 5 - l, s]) & 15))
+                sources.append((1 - l, (s + offset_ref[5 - l, l, s]) & 15))
                 lhs = jnp.concatenate([stack[k][c][at] for at in sources], axis=1)
-                rhs = jnp.concatenate([blocks[index_ref[l, slot, s]] for slot in slots], axis=0)
+                rhs = jnp.concatenate([blocks[index_ref[slot, l, s]] for slot in slots], axis=0)
                 partial[l, s] = product(lhs, rhs)
 
     def finish(k, c, middle, inverse):
@@ -370,8 +313,8 @@
             @pl.loop(0, 16)
             def _(s):
                 slot = 5 + l
-                outer = halo[k][c][l][(s + offset_ref[l, slot - 1, s]) & 15]
-                total = partial[l, s] + product(both_halves(outer), blocks[index_ref[l, slot, s]])
+                outer = halo[k][c][l][(s + offset_ref[slot - 1, l, s]) & 15]
+                total = partial[l, s] + product(both_halves(outer), blocks[index_ref[slot, l, s]])
                 own = field[k][c][l, s]
                 new = (total + (pot_ref[l, pl.ds(s, 1)] - middle) * own) * inverse
                 if k > 0:
@@ -409,20 +352,100 @@
             finish(k, c, middle, inverse)
             if k == 2:
                 rows = pl.ds(pl.multiple_of(128 * st + WIDTH * c, WIDTH), WIDTH)
-                for d in (1, 2, 3):
-                    other = lax.rem(st + d, 4)
-                    copy = send(
-                        chosen[c].at[pl.ds(4 * other, 4)], xt_ref.at[:, :, rows], *sems(), state_peers[d - 1]
-                    )
-                    copies.append(copy)
-                    arrivals.append(copy)
+                for j in range(4) if c == NCH - 1 else [slice(0, 4)]:
+                    for d in (1, 2, 3):
+                        first = 4 * lax.rem(st + d, 4)
+                        part = first + j if c == NCH - 1 else pl.ds(first, 4)
+                        copy = send(chosen[c].at[part], xt_ref.at[j, :, rows], *sems(), state_peers[d - 1])
+                        copies.append(copy)
+                        arrivals.append(copy)
                 for s in range(4):
                     for l in range(2):
                         xt_ref[s, l, rows] = chosen[c][4 * st + s, l]
-    for copy in arrivals:
+    last = len(arrivals) - 12
+    for copy in arrivals[:last]:
         copy.wait_recv()
+    packed = sums[0]
+    for j in range(4):
+        for copy in arrivals[last + 3 * j : last + 3 * j + 3]:
+            copy.wait_recv()
+        hi, lo = halves(jnp.concatenate([xt_ref[j, 0], xt_ref[j, 1]], axis=1))
+        for row in range(4):
+            here, upto = slice(128 * row, 128 * row + 128), 128 * row + 128
+            block = nt(hi[here], hi[:upto]) + (nt(hi[here], lo[:upto]) + nt(lo[here], hi[:upto]))
+            for col in range(row + 1):
+                at = slice(128 * SLOT[row, col], 128 * SLOT[row, col] + 128)
+                piece = block[:, 128 * col : 128 * col + 128]
+                packed[at] = piece if j == 0 else packed[at] + piece
+
+    def meanwhile():
+        @pl.loop(0, 8)
+        def _(q):
+            at = pl.ds(pl.multiple_of(q * 128, 128), 128)
+            for d in range(4):
+                cols = slice(128 * d, 128 * d + 128)
+                xh_ref[at, cols], xl_ref[at, cols] = halves(xt_ref[lax.rem(q, 4), lax.div(q, 4), cols].T)
+
+    sum_everywhere(*sums, gram_ref, sum_peers, sems, copies, meanwhile)
     for copy in copies:
         copy.wait_send()
+
+
+def partners():
+    x, y, z, core = place()
+    return (
+        [device(lax.rem(x + d, 4), y, z, core) for d in (1, 2, 3)],
+        [device(x, lax.rem(y + d, 4), z, core) for d in (1, 2, 3)],
+        [device(x, y, lax.rem(z + d, 8), core) for d in range(1, 8)],
+        [device(x, y, z, 1 - core)],
+    )
+
+
+def sum_everywhere(packed, r1, a1, ra, rb, a2, b2, ra2, rb2, zbuf, gbuf, peers, sems, copies, meanwhile):
+    x, y, z, core = place()
+    x_peers, y_peers, z_peers, core_peers = peers
+
+    def spread(group, piece):
+        started = [send(*piece(d), *sems(), peer) for d, peer in enumerate(group)]
+        copies.extend(started)
+        return started
+
+    def arrived(started):
+        for copy in started:
+            copy.wait_recv()
+
+    def total(own, parts):
+        return (own + parts[0]) + (parts[1] + parts[2])
+
+    arrived(spread(core_peers, lambda d: (packed.at[rows_at((1 - core) * 640, 640)], r1)))
+    a1[...] = packed[rows_at(core * 640, 640)] + r1[...]
+    started = spread(x_peers, lambda d: (a1.at[rows_at(lax.rem(x + d + 1, 4) * 96, 96)], ra.at[d]))
+    started += spread(y_peers, lambda d: (a1.at[rows_at(384 + lax.rem(y + d + 1, 4) * 64, 64)], rb.at[d]))
+    meanwhile()
+    arrived(started)
+    a2[...] = total(a1[rows_at(x * 96, 96)], ra)
+    b2[...] = total(a1[rows_at(384 + y * 64, 64)], rb)
+    started = spread(y_peers, lambda d: (a2.at[rows_at(lax.rem(y + d + 1, 4) * 24, 24)], ra2.at[d]))
+    started += spread(x_peers, lambda d: (b2.at[rows_at(lax.rem(x + d + 1, 4) * 16, 16)], rb2.at[d]))
+    arrived(started)
+    zbuf[z, :24] = total(a2[rows_at(y * 24, 24)], ra2)
+    zbuf[z, 24:] = total(b2[rows_at(x * 16, 16)], rb2)
+    arrived(spread(z_peers, lambda d: (zbuf.at[z], zbuf.at[z])))
+    whole = ((zbuf[0] + zbuf[1]) + (zbuf[2] + zbuf[3])) + ((zbuf[4] + zbuf[5]) + (zbuf[6] + zbuf[7]))
+    own_a = rows_at(core * 640 + x * 96 + y * 24, 24)
+    own_b = rows_at(core * 640 + 384 + y * 64 + x * 16, 16)
+    gbuf[own_a] = whole[:24]
+    gbuf[own_b] = whole[24:]
+    started = spread(y_peers, lambda d: (gbuf.at[own_a], gbuf.at[own_a]))
+    started += spread(x_peers, lambda d: (gbuf.at[own_b], gbuf.at[own_b]))
+    arrived(started)
+    row_a = rows_at(core * 640 + x * 96, 96)
+    row_b = rows_at(core * 640 + 384 + y * 64, 64)
+    started = spread(x_peers, lambda d: (gbuf.at[row_a], gbuf.at[row_a]))
+    started += spread(y_peers, lambda d: (gbuf.at[row_b], gbuf.at[row_b]))
+    arrived(started)
+    half = rows_at(core * 640, 640)
+    arrived(spread(core_peers, lambda d: (gbuf.at[half], gbuf.at[half])))
 
 
 def filtered_rows(start_states, couplings, potential, site_offsets, coupling_index, degrees):
@@ -435,21 +458,29 @@
     scratch += [pltpu.VMEM((16, 128, 256), BF16), pltpu.VMEM((16, 128), F32), pltpu.VMEM((16, 128), F32)]
     scratch += [pltpu.VMEM((n, 16, 128), F32) for n in (8, 4, 2)]
     scratch += [pltpu.VMEM((128, 128), jnp.int32)]
-    scratch += [pltpu.SemaphoreType.DMA((12 * NCH + 11,))] * 2
+    scratch += [pltpu.VMEM((4, 2, 512, 128), F32), pltpu.VMEM((1280, 128), F32)]
+    scratch += [pltpu.VMEM((640, 128), F32), pltpu.VMEM((640, 128), F32)]
+    scratch += [pltpu.VMEM((3, 96, 128), F32), pltpu.VMEM((3, 64, 128), F32)]
+    scratch += [pltpu.VMEM((96, 128), F32), pltpu.VMEM((64, 128), F32)]
+    scratch += [pltpu.VMEM((3, 24, 128), F32), pltpu.VMEM((3, 16, 128), F32), pltpu.VMEM((8, 40, 128), F32)]
+    scratch += [pltpu.SemaphoreType.DMA((COPIES,))] * 2
     return pl.pallas_call(
         filter_kernel,
-        out_shape=jax.ShapeDtypeStruct((4, 2, 512, 128), F32),
+        out_shape=[
+            jax.ShapeDtypeStruct((1280, 128), F32),
+            jax.ShapeDtypeStruct((1024, 512), BF16),
+            jax.ShapeDtypeStruct((1024, 512), BF16),
+        ],
         in_specs=[smem, smem, vmem, vmem, vmem, vmem],
-        out_specs=vmem,
+        out_specs=[vmem] * 3,
         scratch_shapes=scratch,
         compiler_params=pltpu.CompilerParams(collective_id=0, has_side_effects=True, vmem_limit_bytes=VMEM_LIMIT),
         name="filter",
-    )(coupling_index, site_offsets, start_states, couplings, potential, degrees.reshape(1, 128))
+    )(coupling_index.transpose(1, 0, 2), site_offsets.transpose(1, 0, 2), start_states, couplings, potential, degrees.reshape(1, 128))
 
 
 def per_device(start_states, couplings, potential, site_offsets, coupling_index, degrees):
-    xt = filtered_rows(start_states, couplings, potential, site_offsets, coupling_index, degrees)
-    gram, xh, xl = gram_over_devices(xt)
+    gram, xh, xl = filtered_rows(start_states, couplings, potential, site_offsets, coupling_index, degrees)
     return orthonormalised(gram, xh, xl).reshape(2, 4, 128, 512)
 
 

time: 192 us -> 165 us (0.86)
  Pallas kernels: 189 us -> 164 us
  local copies, waits for them, and re-layouts: 2.58 us -> 0 us
    pallas_call x2 -> x1, Pallas kernels: 156 us -> 143 us  [filtered_rows(): pl.pallas_call(filter_kernel, out_shape=[jax.ShapeDtypeStruct((1280, 128)...]
    pallas_call x1, Pallas kernels: 33.1 us -> 21.3 us  [orthonormalised(): pl.pallas_call(factor_kernel, out_shape=jax.ShapeDtypeStruct((1024, 512),...]
    unnamed x2 -> x0, local copies, waits for them, and re-layouts: 2.58 us -> none
where the time goes in v3:
time: 165 us; the launch traced here: 164 us
  Pallas kernels  164 us (99%)
    pallas_call x1, Pallas kernels, filtered_rows(): pl.pallas_call(filter_kernel, out_shape=[jax.ShapeDtypeStruct((1280, 128)...  143 us
    pallas_call x1, Pallas kernels, orthonormalised(): pl.pallas_call(factor_kernel, out_shape=jax.ShapeDtypeStruct((1024, 512),...  21.3 us

profile of v3, /device:TPU:1, one launch (start us, length us, event | category | flops | bytes accessed | tf_op | source)
XLA Modules:
  0.0 164.3 jit_solution(7220179649934221368)
XLA Ops:
  0.0 143.0 %filter.1 = (f32[1280,128]{1,0:T(8,128)}, bf16[1024,512]{1,0:T(8,128)(2,1)}, bf16[1024,512]{1,0:T(8,128)(2,1)}) custom-call(s32[7,2,16]{2,1,0:T(2,128)} %bitcast.6, s32[6,2,16]{2,1,0:T(2,128)} %bitcast.7, f32[2,16,128,128]{3,2,1,0:T(8,128)} %start_ref.1, f32[16,128,128]{2,1,0:T(8,128)} %coup_ref.1, f32[2,16,128]{2,1,0:T(8,128)} %pot_ref.1, s32[1,128]{1,0:T(1,128)} %bitcast.8), custom_call_target="tpu_custom_call" | custom-call | tf_op jit(solution)/shard_map/filter/pallas_call | solution.py:467
  143.0 21.3 %factor.1 = f32[1024,512]{1,0:T(8,128)} custom-call(f32[10,128,128]{2,1,0:T(8,128)} %bitcast.5, bf16[1024,512]{1,0:T(8,128)(2,1)} %get-tuple-element.9.xh, bf16[1024,512]{1,0:T(8,128)(2,1)} %get-tuple-element.10.xl), custom_call_target="tpu_custom_call" | custom-call | tf_op jit(solution)/shard_map/factor/pallas_call | solution.py:167

commit v4 on v3

--- a/solution.py
+++ b/solution.py
@@ -184,7 +184,8 @@
 
 NCH = 2
 WIDTH = 128 // NCH
-COPIES = 6 * NCH + 3 * NCH + 9 + 11 + 33
+PARTS = 2
+COPIES = 6 * NCH + 2 * (PARTS - 1) + 3 * (NCH + PARTS - 1) + 9 + 11 + 33
 
 
 def both_halves(v):
@@ -194,14 +195,24 @@
 
 def product(lhs, rhs):
     full = lax.dot_general(lhs, rhs, (((1,), (0,)), ((), ())), preferred_element_type=F32)
-    return (full[:WIDTH, :128] + full[WIDTH:, :128]) + (full[:WIDTH, 128:] + full[WIDTH:, 128:])
+    half = full.shape[0] // 2
+    return (full[:half, :128] + full[half:, :128]) + (full[:half, 128:] + full[half:, 128:])
+
+
+def parts_of(k, c):
+    return PARTS if (k, c) == (2, NCH - 1) else 1
 
 
 def filter_kernel(index_ref, offset_ref, start_ref, coup_ref, pot_ref, deg_ref, gram_ref, xh_ref, xl_ref, *scratch):
     scratch = iter(scratch)
     field = [[next(scratch) for _ in range(NCH)] for _ in range(3)]
     stack = [[next(scratch) for _ in range(NCH)] for _ in range(3)]
-    halo = [[[next(scratch) for _ in range(2)] for _ in range(NCH)] for _ in range(3)]
+    halo = {}
+    for k in range(3):
+        for c in range(NCH):
+            for part in range(parts_of(k, c)):
+                for l in range(2):
+                    halo[k, c, l, part] = next(scratch)
     partial = next(scratch)
     chosen = [next(scratch) for _ in range(NCH)]
     blocks, row_abs, diag = next(scratch), next(scratch), next(scratch)
@@ -243,10 +254,12 @@
     edge = {}
 
     def send_edge(k, c, l):
-        source = field[k][c].at[l]
-        copy = send(source, halo[k][c][1 - l], *sems(), right if l else left)
-        copies.append(copy)
-        edge[k, c, 1 - l] = copy
+        size = WIDTH // parts_of(k, c)
+        for part in range(parts_of(k, c)):
+            source = field[k][c].at[l, :, size * part : size * part + size]
+            copy = send(source, halo[k, c, 1 - l, part], *sems(), right if l else left)
+            copies.append(copy)
+            edge[k, c, 1 - l, part] = copy
 
     for c in range(NCH):
         send_edge(0, c, 0)
@@ -306,25 +319,27 @@
                 rhs = jnp.concatenate([blocks[index_ref[slot, l, s]] for slot in slots], axis=0)
                 partial[l, s] = product(lhs, rhs)
 
-    def finish(k, c, middle, inverse):
+    def finish(k, c, part, middle, inverse):
+        size = WIDTH // parts_of(k, c)
+        at = slice(size * part, size * part + size)
         for l in range(2):
-            edge[k, c, l].wait_recv()
+            edge[k, c, l, part].wait_recv()
 
             @pl.loop(0, 16)
             def _(s):
                 slot = 5 + l
-                outer = halo[k][c][l][(s + offset_ref[slot - 1, l, s]) & 15]
-                total = partial[l, s] + product(both_halves(outer), blocks[index_ref[slot, l, s]])
-                own = field[k][c][l, s]
+                outer = halo[k, c, l, part][(s + offset_ref[slot - 1, l, s]) & 15]
+                total = partial[l, s, at] + product(both_halves(outer), blocks[index_ref[slot, l, s]])
+                own = field[k][c][l, s, at]
                 new = (total + (pot_ref[l, pl.ds(s, 1)] - middle) * own) * inverse
                 if k > 0:
-                    new = 2.0 * new - field[k - 1][c][l, s]
+                    new = 2.0 * new - field[k - 1][c][l, s, at]
                 if k < 2:
                     field[k + 1][c][l, s] = new
                     stack[k + 1][c][l, s] = both_halves(new)
                 else:
-                    d = degree[WIDTH * c : WIDTH * c + WIDTH]
-                    chosen[c][s, l] = jnp.where(d == 1, field[1][c][l, s], jnp.where(d == 2, own, new))
+                    d = degree[WIDTH * c + size * part : WIDTH * c + size * part + size]
+                    chosen[c][s, l, at] = jnp.where(d == 1, field[1][c][l, s, at], jnp.where(d == 2, own, new))
 
             if k < 2:
                 send_edge(k + 1, c, l)
@@ -349,19 +364,25 @@
         for c in range(NCH):
             if (k, c) != (0, 0):
                 local_part(k, c)
-            finish(k, c, middle, inverse)
-            if k == 2:
-                rows = pl.ds(pl.multiple_of(128 * st + WIDTH * c, WIDTH), WIDTH)
-                for j in range(4) if c == NCH - 1 else [slice(0, 4)]:
+            for part in range(parts_of(k, c)):
+                finish(k, c, part, middle, inverse)
+                if k < 2:
+                    continue
+                size = WIDTH // parts_of(k, c)
+                at = slice(size * part, size * part + size)
+                rows = pl.ds(pl.multiple_of(128 * st + WIDTH * c + size * part, size), size)
+                final = c == NCH - 1 and part == PARTS - 1
+                for j in range(4) if final else [slice(0, 4)]:
                     for d in (1, 2, 3):
                         first = 4 * lax.rem(st + d, 4)
-                        part = first + j if c == NCH - 1 else pl.ds(first, 4)
-                        copy = send(chosen[c].at[part], xt_ref.at[j, :, rows], *sems(), state_peers[d - 1])
+                        sites = first + j if final else pl.ds(first, 4)
+                        source = chosen[c].at[sites, :, at]
+                        copy = send(source, xt_ref.at[j, :, rows], *sems(), state_peers[d - 1])
                         copies.append(copy)
                         arrivals.append(copy)
                 for s in range(4):
                     for l in range(2):
-                        xt_ref[s, l, rows] = chosen[c][4 * st + s, l]
+                        xt_ref[s, l, rows] = chosen[c][4 * st + s, l, at]
     last = len(arrivals) - 12
     for copy in arrivals[:last]:
         copy.wait_recv()
@@ -452,7 +473,9 @@
     vmem, smem = pl.BlockSpec(memory_space=pltpu.VMEM), pl.BlockSpec(memory_space=pltpu.SMEM)
     scratch = [pltpu.VMEM((2, 16, WIDTH, 128), F32)] * (3 * NCH)
     scratch += [pltpu.VMEM((2, 16, 2 * WIDTH, 128), BF16)] * (3 * NCH)
-    scratch += [pltpu.VMEM((16, WIDTH, 128), F32)] * (6 * NCH)
+    for k in range(3):
+        for c in range(NCH):
+            scratch += [pltpu.VMEM((16, WIDTH // parts_of(k, c), 128), F32)] * (2 * parts_of(k, c))
     scratch += [pltpu.VMEM((2, 16, WIDTH, 128), F32)]
     scratch += [pltpu.VMEM((16, 2, WIDTH, 128), F32)] * NCH
     scratch += [pltpu.VMEM((16, 128, 256), BF16), pltpu.VMEM((16, 128), F32), pltpu.VMEM((16, 128), F32)]

time: 165 us -> 165 us (level)
  no operation moved by 1% of the time
where the time goes in v4:
time: 165 us
  Pallas kernels  165 us (100%)
    pallas_call x1, Pallas kernels, filtered_rows(): pl.pallas_call(filter_kernel, out_shape=[jax.ShapeDtypeStruct((1280, 128)...  143 us
    pallas_call x1, Pallas kernels, orthonormalised(): pl.pallas_call(factor_kernel, out_shape=jax.ShapeDtypeStruct((1024, 512),...  21.3 us

profile of v4, /device:TPU:1, one launch (start us, length us, event | category | flops | bytes accessed | tf_op | source)
XLA Modules:
  0.0 164.7 jit_solution(16415646802431554820)
XLA Ops:
  0.0 143.5 %filter.1 = (f32[1280,128]{1,0:T(8,128)}, bf16[1024,512]{1,0:T(8,128)(2,1)}, bf16[1024,512]{1,0:T(8,128)(2,1)}) custom-call(s32[7,2,16]{2,1,0:T(2,128)} %bitcast.6, s32[6,2,16]{2,1,0:T(2,128)} %bitcast.7, f32[2,16,128,128]{3,2,1,0:T(8,128)} %start_ref.1, f32[16,128,128]{2,1,0:T(8,128)} %coup_ref.1, f32[2,16,128]{2,1,0:T(8,128)} %pot_ref.1, s32[1,128]{1,0:T(1,128)} %bitcast.8), custom_call_target="tpu_custom_call" | custom-call | tf_op jit(solution)/shard_map/filter/pallas_call | solution.py:490
  143.5 21.3 %factor.1 = f32[1024,512]{1,0:T(8,128)} custom-call(f32[10,128,128]{2,1,0:T(8,128)} %bitcast.5, bf16[1024,512]{1,0:T(8,128)(2,1)} %get-tuple-element.9.xh, bf16[1024,512]{1,0:T(8,128)(2,1)} %get-tuple-element.10.xl), custom_call_target="tpu_custom_call" | custom-call | tf_op jit(solution)/shard_map/factor/pallas_call | solution.py:167

commit v5 on v4

--- a/solution.py
+++ b/solution.py
@@ -184,8 +184,10 @@
 
 NCH = 2
 WIDTH = 128 // NCH
-PARTS = 2
-COPIES = 6 * NCH + 2 * (PARTS - 1) + 3 * (NCH + PARTS - 1) + 9 + 11 + 33
+PARTS = 1
+AHEAD = 1
+ORDER = [(k, c) for k in range(3) for c in range(NCH)]
+COPIES = 6 * NCH + 2 * (PARTS - 1) + 3 * (NCH + PARTS - 1) + 9 + 11 + 47
 
 
 def both_halves(v):
@@ -240,7 +242,7 @@
     for peer in peers:
         pl.semaphore_signal(barrier, inc=1, device_id=peer, device_id_type=MESH)
 
-    @pl.loop(0, 16)
+    @pl.loop(0, 16, unroll=2)
     def _(s):
         for l in range(2):
             turned = start_ref[l, s].T
@@ -258,16 +260,17 @@
         for part in range(parts_of(k, c)):
             source = field[k][c].at[l, :, size * part : size * part + size]
             copy = send(source, halo[k, c, 1 - l, part], *sems(), right if l else left)
-            copies.append(copy)
+            if ORDER.index((k, c)) + AHEAD >= len(ORDER):
+                copies.append(copy)
             edge[k, c, 1 - l, part] = copy
 
-    for c in range(NCH):
-        send_edge(0, c, 0)
-        send_edge(0, c, 1)
+    for n in range(AHEAD):
+        send_edge(*ORDER[n], 0)
+        send_edge(*ORDER[n], 1)
 
     eye = lax.broadcasted_iota(jnp.int32, (128, 128), 0) == lax.broadcasted_iota(jnp.int32, (128, 128), 1)
 
-    @pl.loop(0, 16)
+    @pl.loop(0, 16, unroll=2)
     def _(n):
         turned = coup_ref[n].T
         row_abs[pl.ds(n, 1)] = jnp.sum(jnp.abs(turned), axis=0, keepdims=True)
@@ -307,7 +310,7 @@
         return best
 
     def local_part(k, c):
-        @pl.loop(0, 16)
+        @pl.loop(0, 16, unroll=4)
         def _(s):
             for l in range(2):
                 sources = [(l, s)]
@@ -325,7 +328,7 @@
         for l in range(2):
             edge[k, c, l, part].wait_recv()
 
-            @pl.loop(0, 16)
+            @pl.loop(0, 16, unroll=8)
             def _(s):
                 slot = 5 + l
                 outer = halo[k, c, l, part][(s + offset_ref[slot - 1, l, s]) & 15]
@@ -341,9 +344,6 @@
                     d = degree[WIDTH * c + size * part : WIDTH * c + size * part + size]
                     chosen[c][s, l, at] = jnp.where(d == 1, field[1][c][l, s, at], jnp.where(d == 2, own, new))
 
-            if k < 2:
-                send_edge(k + 1, c, l)
-
     started = exchange(zb, z, z_peers)
     degree[...] = jnp.broadcast_to(deg_ref[...].astype(F32), (128, 128)).T.astype(jnp.int32)
     local_part(0, 0)
@@ -360,29 +360,35 @@
     inverse = jnp.broadcast_to(2.0 / (upper - cut_edge), (1, 128))
 
     arrivals = []
-    for k in range(3):
-        for c in range(NCH):
-            if (k, c) != (0, 0):
-                local_part(k, c)
-            for part in range(parts_of(k, c)):
-                finish(k, c, part, middle, inverse)
-                if k < 2:
-                    continue
-                size = WIDTH // parts_of(k, c)
-                at = slice(size * part, size * part + size)
-                rows = pl.ds(pl.multiple_of(128 * st + WIDTH * c + size * part, size), size)
-                final = c == NCH - 1 and part == PARTS - 1
-                for j in range(4) if final else [slice(0, 4)]:
-                    for d in (1, 2, 3):
-                        first = 4 * lax.rem(st + d, 4)
-                        sites = first + j if final else pl.ds(first, 4)
-                        source = chosen[c].at[sites, :, at]
-                        copy = send(source, xt_ref.at[j, :, rows], *sems(), state_peers[d - 1])
-                        copies.append(copy)
-                        arrivals.append(copy)
-                for s in range(4):
-                    for l in range(2):
-                        xt_ref[s, l, rows] = chosen[c][4 * st + s, l, at]
+
+    def send_next(n):
+        if n + AHEAD < len(ORDER):
+            for l in range(2):
+                edge[*ORDER[n], 1 - l, 0].wait_send()
+                send_edge(*ORDER[n + AHEAD], l)
+
+    def hand_out(c):
+        rows = pl.ds(pl.multiple_of(128 * st + WIDTH * c, WIDTH), WIDTH)
+        final = c == NCH - 1
+        for j in range(4) if final else [slice(0, 4)]:
+            for d in (1, 2, 3):
+                first = 4 * lax.rem(st + d, 4)
+                source = chosen[c].at[first + j if final else pl.ds(first, 4)]
+                copy = send(source, xt_ref.at[j, :, rows], *sems(), state_peers[d - 1])
+                copies.append(copy)
+                arrivals.append(copy)
+        for s in range(4):
+            for l in range(2):
+                xt_ref[s, l, rows] = chosen[c][4 * st + s, l]
+
+    send_next(0)
+    for n, (k, c) in enumerate(ORDER):
+        finish(k, c, 0, middle, inverse)
+        if k == 2:
+            hand_out(c)
+        if n + 1 < len(ORDER):
+            local_part(*ORDER[n + 1])
+            send_next(n + 1)
     last = len(arrivals) - 12
     for copy in arrivals[:last]:
         copy.wait_recv()
@@ -438,10 +444,28 @@
     def total(own, parts):
         return (own + parts[0]) + (parts[1] + parts[2])
 
-    arrived(spread(core_peers, lambda d: (packed.at[rows_at((1 - core) * 640, 640)], r1)))
-    a1[...] = packed[rows_at(core * 640, 640)] + r1[...]
-    started = spread(x_peers, lambda d: (a1.at[rows_at(lax.rem(x + d + 1, 4) * 96, 96)], ra.at[d]))
-    started += spread(y_peers, lambda d: (a1.at[rows_at(384 + lax.rem(y + d + 1, 4) * 64, 64)], rb.at[d]))
+    def one(source, target, peer):
+        copies.append(send(source, target, *sems(), peer))
+        return copies[-1]
+
+    def piece_a(d):
+        return lax.rem(x + d, 4) * 96
+
+    def piece_b(d):
+        return 384 + lax.rem(y + d, 4) * 64
+
+    pieces = [(piece_a(d), 96, x_peers, ra, d) for d in (1, 2, 3, 0)], [(piece_b(d), 64, y_peers, rb, d) for d in (1, 2, 3, 0)]
+    pieces = [piece for pair in zip(*pieces) for piece in pair]
+    landing = [
+        one(packed.at[rows_at((1 - core) * 640 + at, size)], r1.at[rows_at(at, size)], core_peers[0])
+        for at, size, _, _, _ in pieces
+    ]
+    started = []
+    for copy, (at, size, group, target, d) in zip(landing, pieces):
+        copy.wait_recv()
+        a1[rows_at(at, size)] = packed[rows_at(core * 640 + at, size)] + r1[rows_at(at, size)]
+        if d > 0:
+            started.append(one(a1.at[rows_at(at, size)], target.at[d - 1], group[d - 1]))
     meanwhile()
     arrived(started)
     a2[...] = total(a1[rows_at(x * 96, 96)], ra)
@@ -460,13 +484,20 @@
     started = spread(y_peers, lambda d: (gbuf.at[own_a], gbuf.at[own_a]))
     started += spread(x_peers, lambda d: (gbuf.at[own_b], gbuf.at[own_b]))
     arrived(started)
-    row_a = rows_at(core * 640 + x * 96, 96)
-    row_b = rows_at(core * 640 + 384 + y * 64, 64)
-    started = spread(x_peers, lambda d: (gbuf.at[row_a], gbuf.at[row_a]))
-    started += spread(y_peers, lambda d: (gbuf.at[row_b], gbuf.at[row_b]))
-    arrived(started)
-    half = rows_at(core * 640, 640)
-    arrived(spread(core_peers, lambda d: (gbuf.at[half], gbuf.at[half])))
+
+    def share(at, size, peer):
+        rows = rows_at(core * 640 + at, size)
+        return one(gbuf.at[rows], gbuf.at[rows], peer)
+
+    started = []
+    for d in range(3):
+        started.append((share(x * 96, 96, x_peers[d]), piece_a(3 - d), 96))
+        started.append((share(384 + y * 64, 64, y_peers[d]), piece_b(3 - d), 64))
+    landing = [share(x * 96, 96, core_peers[0]), share(384 + y * 64, 64, core_peers[0])]
+    for copy, at, size in started:
+        copy.wait_recv()
+        landing.append(share(at, size, core_peers[0]))
+    arrived(landing)
 
 
 def filtered_rows(start_states, couplings, potential, site_offsets, coupling_index, degrees):

time: 165 us -> 162 us (0.982)
  Pallas kernels: 165 us -> 161 us
    pallas_call x1, Pallas kernels: 143 us -> 140 us  [filtered_rows(): pl.pallas_call(filter_kernel, out_shape=[jax.ShapeDtypeStruct((1280, 128)...]
where the time goes in v5:
time: 162 us; the launch traced here: 161 us
  Pallas kernels  161 us (99%)
    pallas_call x1, Pallas kernels, filtered_rows(): pl.pallas_call(filter_kernel, out_shape=[jax.ShapeDtypeStruct((1280, 128)...  140 us
    pallas_call x1, Pallas kernels, orthonormalised(): pl.pallas_call(factor_kernel, out_shape=jax.ShapeDtypeStruct((1024, 512),...  21.4 us

profile of v5, /device:TPU:1, one launch (start us, length us, event | category | flops | bytes accessed | tf_op | source)
XLA Modules:
  0.0 161.4 jit_solution(14158775391029031135)
XLA Ops:
  0.0 139.9 %filter.1 = (f32[1280,128]{1,0:T(8,128)}, bf16[1024,512]{1,0:T(8,128)(2,1)}, bf16[1024,512]{1,0:T(8,128)(2,1)}) custom-call(s32[7,2,16]{2,1,0:T(2,128)} %bitcast.6, s32[6,2,16]{2,1,0:T(2,128)} %bitcast.7, f32[2,16,128,128]{3,2,1,0:T(8,128)} %start_ref.1, f32[16,128,128]{2,1,0:T(8,128)} %coup_ref.1, f32[2,16,128]{2,1,0:T(8,128)} %pot_ref.1, s32[1,128]{1,0:T(1,128)} %bitcast.8), custom_call_target="tpu_custom_call" | custom-call | tf_op jit(solution)/shard_map/filter/pallas_call | solution.py:521
  139.9 21.4 %factor.1 = f32[1024,512]{1,0:T(8,128)} custom-call(f32[10,128,128]{2,1,0:T(8,128)} %bitcast.5, bf16[1024,512]{1,0:T(8,128)(2,1)} %get-tuple-element.9.xh, bf16[1024,512]{1,0:T(8,128)(2,1)} %get-tuple-element.10.xl), custom_call_target="tpu_custom_call" | custom-call | tf_op jit(solution)/shard_map/factor/pallas_call | solution.py:167

commit v6 on v5

--- a/solution.py
+++ b/solution.py
@@ -1,3 +1,5 @@
+import functools
+
 import jax
 import jax.numpy as jnp
 from jax import lax
@@ -74,7 +76,7 @@
     return lax.dot_general(lhs, rhs, (((1,), (0,)), ((), ())), preferred_element_type=F32)
 
 
-def eliminate(work):
+def eliminate(work, others):
     row = lax.broadcasted_iota(jnp.int32, (16, 128), 0)
 
     def spread(v, rows=16):
@@ -114,6 +116,8 @@
         lo = PANEL * p
         for t in range(PANEL // 16):
             steps(lo + 16 * t, PANEL // 16 - t)
+            if others:
+                others.pop(0)()
         if lo + PANEL < 128:
             h, m, l = thirds(work[lo : lo + PANEL, :])
             lhs = jnp.concatenate([h[:, :128], h[:, :128], m[:, :128], m[:, :128], h[:, :128], l[:, :128]], axis=0).astype(BF16)
@@ -125,41 +129,50 @@
 PANEL = 32
 
 
-def factor_kernel(g_ref, xh, xl, out_ref, blocks, work, low, inv, ih, il):
+def factor_kernel(g_ref, xh, xl, out_ref, blocks, work, low, inv):
     blocks[...] = g_ref[...]
     inv[...] = jnp.zeros_like(inv)
     eye = (lax.broadcasted_iota(jnp.int32, (128, 128), 0) == lax.broadcasted_iota(jnp.int32, (128, 128), 1)).astype(F32)
 
-    @pl.loop(0, 4)
-    def _(k):
-        work[:, :128] = blocks[lax.div(k * (k + 1), 2) + k]
-        work[:, 128:] = eye
-        eliminate(work)
-        for n in range(4):
-
-            @pl.when(k == n)
-            def _():
-                here = slice(128 * n, 128 * n + 128)
-                w = work[:, 128:]
-                inv[here, here] = w
-                if n > 0:
-                    known = dot_nn(low[here, : 128 * n], inv[: 128 * n, : 128 * n])
-                    inv[here, : 128 * n] = -dot_nn(w, known)
-                for i in range(n + 1, 4):
-                    low[128 * i : 128 * i + 128, here] = dot_nt(blocks[SLOT[i, n]], w)
-                for j in range(n + 1, 4):
-                    for i in range(j, 4):
-                        blocks[SLOT[i, j]] = blocks[SLOT[i, j]] - dot_nt(
-                            low[128 * i : 128 * i + 128, here], low[128 * j : 128 * j + 128, here]
-                        )
-
-    ih[...], il[...] = halves(inv[...])
-
-    for i in range(4):
-        here, upto = slice(128 * i, 128 * i + 128), 128 * i + 128
-        a, b = xh[:, :upto], xl[:, :upto]
-        u, v = ih[here, :upto], il[here, :upto]
-        out_ref[:, here] = nt(a, u) + (nt(a, v) + nt(b, u))
+    def lower_block(i, n):
+        low[128 * i : 128 * i + 128, 128 * n : 128 * n + 128] = dot_nt(blocks[SLOT[i, n]], work[n, :, 128:])
+
+    def update(i, j, n):
+        cols = slice(128 * n, 128 * n + 128)
+        blocks[SLOT[i, j]] = blocks[SLOT[i, j]] - dot_nt(
+            low[128 * i : 128 * i + 128, cols], low[128 * j : 128 * j + 128, cols]
+        )
+
+    def inverse_row(n):
+        here = slice(128 * n, 128 * n + 128)
+        w = work[n, :, 128:]
+        inv[here, here] = w
+        if n > 0:
+            inv[here, : 128 * n] = -dot_nn(w, dot_nn(low[here, : 128 * n], inv[: 128 * n, : 128 * n]))
+
+    def product_block(n, part):
+        here, upto, rows = slice(128 * n, 128 * n + 128), 128 * n + 128, slice(512 * part, 512 * part + 512)
+        u, v = halves(inv[here, :upto])
+        a, b = xh[rows, :upto], xl[rows, :upto]
+        out_ref[rows, here] = nt(a, u) + (nt(a, v) + nt(b, u))
+
+    call = functools.partial
+    others = []
+    for n in range(4):
+        mine = work.at[n]
+        mine[:, :128] = blocks[SLOT[n, n]]
+        mine[:, 128:] = eye
+        eliminate(mine, others)
+        while others:
+            others.pop(0)()
+        if n < 3:
+            lower_block(n + 1, n)
+            update(n + 1, n + 1, n)
+        others = [call(lower_block, i, n) for i in range(n + 2, 4)]
+        others += [call(update, i, j, n) for j in range(n + 1, 4) for i in range(max(j, n + 2), 4)]
+        others += [call(inverse_row, n), call(product_block, n, 0), call(product_block, n, 1)]
+    for other in others:
+        other()
 
 
 def orthonormalised(packed, xh, xl):
@@ -171,11 +184,9 @@
         out_specs=vmem,
         scratch_shapes=[
             pltpu.VMEM((10, 128, 128), F32),
-            pltpu.VMEM((128, 256), F32),
+            pltpu.VMEM((4, 128, 256), F32),
             pltpu.VMEM((512, 512), F32),
             pltpu.VMEM((512, 512), F32),
-            pltpu.VMEM((512, 512), BF16),
-            pltpu.VMEM((512, 512), BF16),
         ],
         compiler_params=pltpu.CompilerParams(vmem_limit_bytes=VMEM_LIMIT),
         name="factor",

time: 162 us -> 158 us (0.975)
  Pallas kernels: 161 us -> 158 us
    pallas_call x1, Pallas kernels: 21.4 us -> 18.3 us  [orthonormalised(): pl.pallas_call(factor_kernel, out_shape=jax.ShapeDtypeStruct((1024, 512),...]
where the time goes in v6:
time: 158 us
  Pallas kernels  158 us (100%)
    pallas_call x1, Pallas kernels, filtered_rows(): pl.pallas_call(filter_kernel, out_shape=[jax.ShapeDtypeStruct((1280, 128)...  140 us
    pallas_call x1, Pallas kernels, orthonormalised(): pl.pallas_call(factor_kernel, out_shape=jax.ShapeDtypeStruct((1024, 512),...  18.3 us

profile of v6, /device:TPU:1, one launch (start us, length us, event | category | flops | bytes accessed | tf_op | source)
XLA Modules:
  0.0 158.2 jit_solution(11273722788961074181)
XLA Ops:
  0.0 139.9 %filter.1 = (f32[1280,128]{1,0:T(8,128)}, bf16[1024,512]{1,0:T(8,128)(2,1)}, bf16[1024,512]{1,0:T(8,128)(2,1)}) custom-call(s32[7,2,16]{2,1,0:T(2,128)} %bitcast.6, s32[6,2,16]{2,1,0:T(2,128)} %bitcast.7, f32[2,16,128,128]{3,2,1,0:T(8,128)} %start_ref.1, f32[16,128,128]{2,1,0:T(8,128)} %coup_ref.1, f32[2,16,128]{2,1,0:T(8,128)} %pot_ref.1, s32[1,128]{1,0:T(1,128)} %bitcast.8), custom_call_target="tpu_custom_call" | custom-call | tf_op jit(solution)/shard_map/filter/pallas_call | solution.py:532
  139.9 18.3 %factor.1 = f32[1024,512]{1,0:T(8,128)} custom-call(f32[10,128,128]{2,1,0:T(8,128)} %bitcast.5, bf16[1024,512]{1,0:T(8,128)(2,1)} %get-tuple-element.9.xh, bf16[1024,512]{1,0:T(8,128)(2,1)} %get-tuple-element.10.xl), custom_call_target="tpu_custom_call" | custom-call | tf_op jit(solution)/shard_map/factor/pallas_call | solution.py:180

commit v7 on v6

--- a/solution.py
+++ b/solution.py
@@ -416,8 +416,8 @@
                 piece = block[:, 128 * col : 128 * col + 128]
                 packed[at] = piece if j == 0 else packed[at] + piece
 
-    def meanwhile():
-        @pl.loop(0, 8)
+    def meanwhile(part):
+        @pl.loop(4 * part, 4 * part + 4, unroll=2)
         def _(q):
             at = pl.ds(pl.multiple_of(q * 128, 128), 128)
             for d in range(4):
@@ -477,7 +477,7 @@
         a1[rows_at(at, size)] = packed[rows_at(core * 640 + at, size)] + r1[rows_at(at, size)]
         if d > 0:
             started.append(one(a1.at[rows_at(at, size)], target.at[d - 1], group[d - 1]))
-    meanwhile()
+    meanwhile(0)
     arrived(started)
     a2[...] = total(a1[rows_at(x * 96, 96)], ra)
     b2[...] = total(a1[rows_at(384 + y * 64, 64)], rb)
@@ -486,7 +486,9 @@
     arrived(started)
     zbuf[z, :24] = total(a2[rows_at(y * 24, 24)], ra2)
     zbuf[z, 24:] = total(b2[rows_at(x * 16, 16)], rb2)
-    arrived(spread(z_peers, lambda d: (zbuf.at[z], zbuf.at[z])))
+    started = spread(z_peers, lambda d: (zbuf.at[z], zbuf.at[z]))
+    meanwhile(1)
+    arrived(started)
     whole = ((zbuf[0] + zbuf[1]) + (zbuf[2] + zbuf[3])) + ((zbuf[4] + zbuf[5]) + (zbuf[6] + zbuf[7]))
     own_a = rows_at(core * 640 + x * 96 + y * 24, 24)
     own_b = rows_at(core * 640 + 384 + y * 64 + x * 16, 16)

time: 158 us -> 158 us (level)
  no operation moved by 1% of the time
where the time goes in v7:
time: 158 us
  Pallas kernels  158 us (100%)
    pallas_call x1, Pallas kernels, filtered_rows(): pl.pallas_call(filter_kernel, out_shape=[jax.ShapeDtypeStruct((1280, 128)...  140 us
    pallas_call x1, Pallas kernels, orthonormalised(): pl.pallas_call(factor_kernel, out_shape=jax.ShapeDtypeStruct((1024, 512),...  18.3 us

profile of v7, /device:TPU:1, one launch (start us, length us, event | category | flops | bytes accessed | tf_op | source)
XLA Modules:
  0.0 158.2 jit_solution(17740329358032249087)
XLA Ops:
  0.0 139.9 %filter.1 = (f32[1280,128]{1,0:T(8,128)}, bf16[1024,512]{1,0:T(8,128)(2,1)}, bf16[1024,512]{1,0:T(8,128)(2,1)}) custom-call(s32[7,2,16]{2,1,0:T(2,128)} %bitcast.6, s32[6,2,16]{2,1,0:T(2,128)} %bitcast.7, f32[2,16,128,128]{3,2,1,0:T(8,128)} %start_ref.1, f32[16,128,128]{2,1,0:T(8,128)} %coup_ref.1, f32[2,16,128]{2,1,0:T(8,128)} %pot_ref.1, s32[1,128]{1,0:T(1,128)} %bitcast.8), custom_call_target="tpu_custom_call" | custom-call | tf_op jit(solution)/shard_map/filter/pallas_call | solution.py:534
  139.9 18.3 %factor.1 = f32[1024,512]{1,0:T(8,128)} custom-call(f32[10,128,128]{2,1,0:T(8,128)} %bitcast.5, bf16[1024,512]{1,0:T(8,128)(2,1)} %get-tuple-element.9.xh, bf16[1024,512]{1,0:T(8,128)(2,1)} %get-tuple-element.10.xl), custom_call_target="tpu_custom_call" | custom-call | tf_op jit(solution)/shard_map/factor/pallas_call | solution.py:180

commit v8 on v6

--- a/solution.py
+++ b/solution.py
@@ -193,12 +193,12 @@
     )(packed.reshape(10, 128, 128), xh, xl)
 
 
-NCH = 2
+NCH = 4
 WIDTH = 128 // NCH
 PARTS = 1
-AHEAD = 1
+AHEAD = 2
 ORDER = [(k, c) for k in range(3) for c in range(NCH)]
-COPIES = 6 * NCH + 2 * (PARTS - 1) + 3 * (NCH + PARTS - 1) + 9 + 11 + 47
+COPIES = 6 * NCH + 2 * (PARTS - 1) + 3 * (NCH + PARTS - 1) + 9 + 14 + 47
 
 
 def both_halves(v):
@@ -226,10 +226,10 @@
             for part in range(parts_of(k, c)):
                 for l in range(2):
                     halo[k, c, l, part] = next(scratch)
-    partial = next(scratch)
+    partial = [next(scratch) for _ in range(NCH)]
     chosen = [next(scratch) for _ in range(NCH)]
     blocks, row_abs, diag = next(scratch), next(scratch), next(scratch)
-    zb, xb, yb = next(scratch), next(scratch), next(scratch)
+    zb, plane_buf = next(scratch), next(scratch)
     degree = next(scratch)
     xt_ref = next(scratch)
     sums = [next(scratch) for _ in range(10)]
@@ -241,28 +241,18 @@
         return send_sems.at[i], recv_sems.at[i]
 
     b, st = lax.axis_index("blk"), lax.axis_index("states")
-    z, xx, ylo = lax.rem(b, 8), lax.rem(lax.div(b, 8), 4), lax.div(b, 32)
+    z = lax.rem(b, 8)
     left, right = (lax.rem(b + 63, 64), st), (lax.rem(b + 1, 64), st)
     z_peers = [(b - z + lax.rem(z + d, 8), st) for d in range(1, 8)]
-    x_peers = [(b - xx * 8 + lax.rem(xx + d, 4) * 8, st) for d in range(1, 4)]
-    y_peer = (lax.rem(b + 32, 64), st)
+    plane = lax.div(b, 8)
+    plane_peers = [(lax.rem(plane + d, 8) * 8 + z, st) for d in range(1, 8)]
     state_peers = [(b, lax.rem(st + d, 4)) for d in range(1, 4)]
     sum_peers = partners()
-    peers = [left, right, y_peer] + z_peers + x_peers + state_peers + [peer for group in sum_peers for peer in group]
+    peers = [left, right] + z_peers + plane_peers + state_peers + [peer for group in sum_peers for peer in group]
     barrier = pltpu.get_barrier_semaphore()
     for peer in peers:
         pl.semaphore_signal(barrier, inc=1, device_id=peer, device_id_type=MESH)
 
-    @pl.loop(0, 16, unroll=2)
-    def _(s):
-        for l in range(2):
-            turned = start_ref[l, s].T
-            for c in range(NCH):
-                part = turned[WIDTH * c : WIDTH * c + WIDTH]
-                field[0][c][l, s] = part
-                stack[0][c][l, s] = both_halves(part)
-
-    pl.semaphore_wait(barrier, len(peers))
     copies = []
     edge = {}
 
@@ -275,9 +265,6 @@
                 copies.append(copy)
             edge[k, c, 1 - l, part] = copy
 
-    for n in range(AHEAD):
-        send_edge(*ORDER[n], 0)
-        send_edge(*ORDER[n], 1)
 
     eye = lax.broadcasted_iota(jnp.int32, (128, 128), 0) == lax.broadcasted_iota(jnp.int32, (128, 128), 1)
 
@@ -331,7 +318,7 @@
                 sources.append((1 - l, (s + offset_ref[5 - l, l, s]) & 15))
                 lhs = jnp.concatenate([stack[k][c][at] for at in sources], axis=1)
                 rhs = jnp.concatenate([blocks[index_ref[slot, l, s]] for slot in slots], axis=0)
-                partial[l, s] = product(lhs, rhs)
+                partial[c][l, s] = product(lhs, rhs)
 
     def finish(k, c, part, middle, inverse):
         size = WIDTH // parts_of(k, c)
@@ -343,7 +330,7 @@
             def _(s):
                 slot = 5 + l
                 outer = halo[k, c, l, part][(s + offset_ref[slot - 1, l, s]) & 15]
-                total = partial[l, s, at] + product(both_halves(outer), blocks[index_ref[slot, l, s]])
+                total = partial[c][l, s, at] + product(both_halves(outer), blocks[index_ref[slot, l, s]])
                 own = field[k][c][l, s, at]
                 new = (total + (pot_ref[l, pl.ds(s, 1)] - middle) * own) * inverse
                 if k > 0:
@@ -355,15 +342,27 @@
                     d = degree[WIDTH * c + size * part : WIDTH * c + size * part + size]
                     chosen[c][s, l, at] = jnp.where(d == 1, field[1][c][l, s, at], jnp.where(d == 2, own, new))
 
+    pl.semaphore_wait(barrier, len(peers))
     started = exchange(zb, z, z_peers)
+
+    @pl.loop(0, 16, unroll=2)
+    def _(s):
+        for l in range(2):
+            turned = start_ref[l, s].T
+            for c in range(NCH):
+                part = turned[WIDTH * c : WIDTH * c + WIDTH]
+                field[0][c][l, s] = part
+                stack[0][c][l, s] = both_halves(part)
+
+    plane_buf[plane] = merged(zb, started)
+    started = exchange(plane_buf, plane, plane_peers)
+    for n in range(AHEAD):
+        send_edge(*ORDER[n], 0)
+        send_edge(*ORDER[n], 1)
     degree[...] = jnp.broadcast_to(deg_ref[...].astype(F32), (128, 128)).T.astype(jnp.int32)
-    local_part(0, 0)
-    xb[xx] = merged(zb, started)
-    started = exchange(xb, xx, x_peers)
-    best = merged(xb, started)
-    yb[ylo] = best
-    started = exchange(yb, ylo, [y_peer])
-    best = merged(yb, started)
+    for c in range(NCH):
+        local_part(0, c)
+    best = merged(plane_buf, started)
     upper = jnp.max(best[:8], axis=1, keepdims=True)[:1]
     lower = -jnp.max(best[8:], axis=1, keepdims=True)[:1]
     cut_edge = lower + cut_share * (upper - lower)
@@ -392,13 +391,15 @@
             for l in range(2):
                 xt_ref[s, l, rows] = chosen[c][4 * st + s, l]
 
-    send_next(0)
     for n, (k, c) in enumerate(ORDER):
+        if n == 0:
+            send_next(0)
         finish(k, c, 0, middle, inverse)
         if k == 2:
             hand_out(c)
+        else:
+            local_part(k + 1, c)
         if n + 1 < len(ORDER):
-            local_part(*ORDER[n + 1])
             send_next(n + 1)
     last = len(arrivals) - 12
     for copy in arrivals[:last]:
@@ -518,10 +519,10 @@
     for k in range(3):
         for c in range(NCH):
             scratch += [pltpu.VMEM((16, WIDTH // parts_of(k, c), 128), F32)] * (2 * parts_of(k, c))
-    scratch += [pltpu.VMEM((2, 16, WIDTH, 128), F32)]
+    scratch += [pltpu.VMEM((2, 16, WIDTH, 128), F32)] * NCH
     scratch += [pltpu.VMEM((16, 2, WIDTH, 128), F32)] * NCH
     scratch += [pltpu.VMEM((16, 128, 256), BF16), pltpu.VMEM((16, 128), F32), pltpu.VMEM((16, 128), F32)]
-    scratch += [pltpu.VMEM((n, 16, 128), F32) for n in (8, 4, 2)]
+    scratch += [pltpu.VMEM((8, 16, 128), F32)] * 2
     scratch += [pltpu.VMEM((128, 128), jnp.int32)]
     scratch += [pltpu.VMEM((4, 2, 512, 128), F32), pltpu.VMEM((1280, 128), F32)]
     scratch += [pltpu.VMEM((640, 128), F32), pltpu.VMEM((640, 128), F32)]

time: 158 us -> 162 us (1.025)
  Pallas kernels: 158 us -> 161 us
    pallas_call x1, Pallas kernels: 140 us -> 143 us  [filtered_rows(): pl.pallas_call(filter_kernel, out_shape=[jax.ShapeDtypeStruct((1280, 128)...]
where the time goes in v8:
time: 162 us; the launch traced here: 161 us
  Pallas kernels  161 us (99%)
    pallas_call x1, Pallas kernels, filtered_rows(): pl.pallas_call(filter_kernel, out_shape=[jax.ShapeDtypeStruct((1280, 128)...  143 us
    pallas_call x1, Pallas kernels, orthonormalised(): pl.pallas_call(factor_kernel, out_shape=jax.ShapeDtypeStruct((1024, 512),...  18.3 us

profile of v8, /device:TPU:1, one launch (start us, length us, event | category | flops | bytes accessed | tf_op | source)
XLA Modules:
  0.0 161.4 jit_solution(9059357604913565762)
XLA Ops:
  0.0 143.1 %filter.1 = (f32[1280,128]{1,0:T(8,128)}, bf16[1024,512]{1,0:T(8,128)(2,1)}, bf16[1024,512]{1,0:T(8,128)(2,1)}) custom-call(s32[7,2,16]{2,1,0:T(2,128)} %bitcast.6, s32[6,2,16]{2,1,0:T(2,128)} %bitcast.7, f32[2,16,128,128]{3,2,1,0:T(8,128)} %start_ref.1, f32[16,128,128]{2,1,0:T(8,128)} %coup_ref.1, f32[2,16,128]{2,1,0:T(8,128)} %pot_ref.1, s32[1,128]{1,0:T(1,128)} %bitcast.8), custom_call_target="tpu_custom_call" | custom-call | tf_op jit(solution)/shard_map/filter/pallas_call | solution.py:533
  143.1 18.3 %factor.1 = f32[1024,512]{1,0:T(8,128)} custom-call(f32[10,128,128]{2,1,0:T(8,128)} %bitcast.5, bf16[1024,512]{1,0:T(8,128)(2,1)} %get-tuple-element.9.xh, bf16[1024,512]{1,0:T(8,128)(2,1)} %get-tuple-element.10.xl), custom_call_target="tpu_custom_call" | custom-call | tf_op jit(solution)/shard_map/factor/pallas_call | solution.py:180
